TPU v7x, 256 devices: a whole 4x4x8 slice. The times are simulated.
256 devices in a mesh: dp: 8 (over z), own: 32 (over x, y, core).
Axes of the slice: x: 4, y: 4, z: 8, core: 2. Of those that a mesh axis runs over, the one named last changes fastest.
Arguments:
- signals: bfloat16 [65536, 384], P(('dp', 'own')), may hold values from -6 to 6
- cotangent: bfloat16 [65536, 384], P(('dp', 'own')), may hold values from -6 to 6
- row_insertion: int32 [65536], P(('dp', 'own')), may hold values from 0 to 63, as said below
- touched: int32 [256, 4], replicated, may hold values from 0 to 63, as said below
- slot_map: int32 [64], replicated, may hold values from 0 to 63, each once
- weights: bfloat16 [64, 2, 384, 1024], P(None, None, 'own'), may hold values from -0.3125 to 0.3125
- moment1: float32 [64, 2, 384, 1024], P(None, None, 'own', 'dp'), may hold values from -25.6 to 25.6
- moment2: float32 [64, 2, 384, 1024], P(None, None, 'own', 'dp'), may hold values from 0.2048 to 6.144
Outputs:
- predicted: bfloat16 [65536, 384], P(('dp', 'own'))
- new_weights: bfloat16 [64, 2, 384, 1024], P(None, None, 'own')
- new_moment1: float32 [64, 2, 384, 1024], P(None, None, 'own', 'dp')
- new_moment2: float32 [64, 2, 384, 1024], P(None, None, 'own', 'dp')
Inputs may be any that keep to these rules, and one draw needn't show every extreme that they name: `row_insertion`: device d (dp index times the size of own plus own index) holds rows d * 256 to (d + 1) * 256 - 1; their insertions are all in row d of touched; at most 128 rows of one device name the same insertion, and on every device one insertion is named by exactly 128 rows. `touched`: each row lists 4 different insertions.
All inputs are finite; a program needn't handle non-finite values.
Results may differ from a plain program's by a relative error of at most 0.0049.
Values may be sent and summed in bfloat16 or wider, within the bound.
A program may use at most 128 MiB of HBM per device.

v0:
```python
import functools
import math

import jax
import jax.numpy as jnp
from jax import lax
from jax.experimental import pallas as pl
from jax.experimental.pallas import tpu as pltpu
from jax.sharding import PartitionSpec as P

SITES = 384
WIDTH = 1024
TOUCH = 4
CAP = 128

MESH = pl.DeviceIdType.MESH

def _a2a_kernel(n_dp, n_own, full, x_ref, o_ref, send_sems, recv_sems, local_sem):
    dp_at = lax.axis_index("dp")
    own_at = lax.axis_index("own")
    if full:
        n = n_dp * n_own
        me = dp_at * n_own + own_at
        def dev(k):
            return (k // n_own, k % n_own)
    else:
        n = n_own
        me = own_at
        def dev(k):
            return (dp_at, k)
    barrier = pltpu.get_barrier_semaphore()

    def greet(i, c):
        peer = lax.rem(me + i, n)
        pl.semaphore_signal(barrier, 1, device_id=dev(peer), device_id_type=MESH)
        return c

    lax.fori_loop(1, n, greet, 0)
    pl.semaphore_wait(barrier, n - 1)
    local = pltpu.make_async_copy(x_ref.at[me], o_ref.at[me], local_sem)
    local.start()

    def send(i, c):
        peer = lax.rem(me + i, n)
        pltpu.make_async_remote_copy(
            src_ref=x_ref.at[peer], dst_ref=o_ref.at[me],
            send_sem=send_sems.at[peer], recv_sem=recv_sems.at[me],
            device_id=dev(peer), device_id_type=MESH,
        ).start()
        return c

    lax.fori_loop(1, n, send, 0)

    def finish(i, c):
        peer = lax.rem(me + i, n)
        src = lax.rem(me + n - i, n)
        pltpu.make_async_remote_copy(
            src_ref=x_ref.at[peer], dst_ref=o_ref.at[src],
            send_sem=send_sems.at[peer], recv_sem=recv_sems.at[src],
            device_id=dev(peer), device_id_type=MESH,
        ).wait_send()
        pltpu.make_async_remote_copy(
            src_ref=x_ref.at[peer], dst_ref=o_ref.at[src],
            send_sem=send_sems.at[peer], recv_sem=recv_sems.at[src],
            device_id=dev(src), device_id_type=MESH,
        ).wait_recv()
        return c

    lax.fori_loop(1, n, finish, 0)
    local.wait()


def exchange(x, n_dp, n_own, full, cid):
    n = x.shape[0]
    return pl.pallas_call(
        functools.partial(_a2a_kernel, n_dp, n_own, full),
        out_shape=jax.ShapeDtypeStruct(x.shape, x.dtype),
        in_specs=[pl.BlockSpec(memory_space=pl.ANY)],
        out_specs=pl.BlockSpec(memory_space=pl.ANY),
        scratch_shapes=[
            pltpu.SemaphoreType.DMA((n,)),
            pltpu.SemaphoreType.DMA((n,)),
            pltpu.SemaphoreType.DMA,
        ],
        compiler_params=pltpu.CompilerParams(collective_id=cid, has_side_effects=True),
    )(x)


gelu_coef = math.sqrt(2.0 / math.pi)
cubic_coef = 0.044715
learn_rate = 0.01
highest = lax.Precision.HIGHEST


def gelu_parts(preact):
    tanh_input = gelu_coef * (preact + cubic_coef * preact * preact * preact)
    tangent = jnp.tanh(tanh_input)
    gelu_val = 0.5 * preact * (1.0 + tangent)
    slopes = 0.5 * (1.0 + tangent) + 0.5 * preact * (1.0 - tangent * tangent) * gelu_coef * (
        1.0 + 3.0 * cubic_coef * preact * preact
    )
    return (gelu_val, slopes)


def dispatch(row_ids, listed):
    match_table = (row_ids[:, None] == listed[None, :]).astype(jnp.int32)
    running = jnp.cumsum(match_table, axis=0) - 1
    slot_of = jnp.sum(match_table * jnp.arange(listed.shape[0], dtype=jnp.int32)[None, :], axis=1)
    within = jnp.sum(match_table * running, axis=1)
    return slot_of * CAP + within


def adam_step(params, moment_one, moment_two, gradient):
    moment_one = 0.9 * moment_one + 0.1 * gradient
    moment_two = 0.999 * moment_two + 0.001 * gradient * gradient
    correct_one = 1.0 - 0.9**10
    correct_two = 1.0 - 0.999**10
    updated = params - learn_rate * (moment_one / correct_one) / (
        jnp.sqrt(moment_two / correct_two) + 1e-08
    )
    return (updated.astype(jnp.bfloat16), moment_one, moment_two)


def sum_by_insertion(item_rows, arrived_grad, number):
    one_hot = (jnp.arange(number, dtype=jnp.int32)[:, None] == item_rows[None, :]).astype(
        arrived_grad.dtype
    )
    flat_grad = arrived_grad.reshape(item_rows.shape[0], -1)
    return jnp.dot(one_hot, flat_grad, preferred_element_type=jnp.float32)


def shards(signals, cotangent, row_insertion, touched, slot_map, weights, moment1, moment2):
    n_own = lax.axis_size("own")
    n_dp = lax.axis_size("dp")
    dp_at = lax.axis_index("dp")
    own_at = lax.axis_index("own")
    number = weights.shape[0]
    piece_rows = weights.shape[2]
    width_part = moment1.shape[3]
    pairs = n_dp * TOUCH
    stored = jnp.sum(
        jnp.where(
            touched[:, :, None] == jnp.arange(number, dtype=jnp.int32)[None, None, :],
            slot_map[None, None, :],
            0,
        ),
        axis=2,
    )
    peer_rows = stored.reshape(n_dp, n_own, TOUCH).transpose(1, 0, 2).reshape(-1)
    my_list = lax.dynamic_index_in_dim(touched, dp_at * n_own + own_at, 0, keepdims=False)
    places = dispatch(row_insertion, my_list)
    stacked = (
        jnp.zeros((TOUCH * CAP, 2 * SITES), signals.dtype)
        .at[places]
        .set(jnp.concatenate([signals, cotangent], axis=1))
    )
    stacked = lax.all_gather(stacked.reshape(TOUCH, CAP, 2 * SITES), "dp", axis=0, tiled=True)
    stacked = stacked.reshape(pairs, CAP, 2 * SITES)
    sig_slots = stacked[:, :, :SITES]
    cot_slots = stacked[:, :, SITES:]
    my_width = lax.dynamic_slice_in_dim(weights, dp_at * width_part, width_part, 3)
    pick = (peer_rows[:, None] == jnp.arange(number, dtype=jnp.int32)[None, :]).astype(weights.dtype)
    outgoing = jnp.dot(
        pick, my_width.reshape(number, -1), preferred_element_type=jnp.float32
    ).astype(weights.dtype)
    outgoing = outgoing.reshape(n_own, pairs, 2 * piece_rows * width_part)
    arrived = lax.all_to_all(outgoing, "own", split_axis=0, concat_axis=0, tiled=True)
    arrived = arrived.reshape(n_own, pairs, 2, piece_rows, width_part)
    arrived = arrived.transpose(1, 2, 0, 3, 4).reshape(pairs, 2, SITES, width_part)
    read_in = arrived[:, 0]
    read_out = arrived[:, 1]
    preact = jnp.einsum("kcs,ksw->kcw", sig_slots, read_in, preferred_element_type=jnp.float32)
    gelu_val, slopes = gelu_parts(preact)
    hidden = gelu_val.astype(jnp.bfloat16)
    pred_part = jnp.einsum("kcw,ksw->kcs", hidden, read_out, preferred_element_type=jnp.float32)
    back_hidden = jnp.einsum(
        "kcs,ksw->kcw", cot_slots, read_out, preferred_element_type=jnp.float32
    )
    back_pre = (back_hidden * slopes).astype(jnp.bfloat16)
    grad_in = jnp.einsum("kcs,kcw->ksw", sig_slots, back_pre, preferred_element_type=jnp.float32)
    grad_out = jnp.einsum("kcs,kcw->ksw", cot_slots, hidden, preferred_element_type=jnp.float32)
    grads = jnp.stack([grad_in, grad_out], axis=1).astype(jnp.bfloat16)
    pred_part, grads = lax.optimization_barrier((pred_part, grads))
    pred_slots = lax.psum_scatter(pred_part, "dp", scatter_dimension=0, tiled=True)
    pieces = grads.reshape(pairs, 2, n_own, piece_rows, width_part).transpose(2, 0, 1, 3, 4)
    pieces = pieces.reshape(n_own, pairs, 2 * piece_rows * width_part)
    arrived_grad = lax.all_to_all(pieces, "own", split_axis=0, concat_axis=0, tiled=True)
    arrived_grad, pred_slots = lax.optimization_barrier((arrived_grad, pred_slots))
    pred_slots = pred_slots.astype(jnp.bfloat16)
    table = sum_by_insertion(peer_rows, arrived_grad, number).reshape(
        number, 2, piece_rows, width_part
    )
    own_params = my_width.astype(jnp.float32)
    fresh_part, new_moment1, new_moment2 = adam_step(own_params, moment1, moment2, table)
    new_weights = lax.all_gather(fresh_part, "dp", axis=0, tiled=False)
    new_weights = new_weights.transpose(1, 2, 3, 0, 4).reshape(weights.shape)
    predicted = pred_slots.reshape(TOUCH * CAP, SITES)[places]
    return (predicted, new_weights, new_moment1, new_moment2)


def solution(mesh):
    in_specs = (
        P(("dp", "own"), None),
        P(("dp", "own"), None),
        P(("dp", "own")),
        P(),
        P(),
        P(None, None, "own", None),
        P(None, None, "own", "dp"),
        P(None, None, "own", "dp"),
    )
    out_specs = (
        P(("dp", "own"), None),
        P(None, None, "own", None),
        P(None, None, "own", "dp"),
        P(None, None, "own", "dp"),
    )
    return jax.shard_map(shards, mesh=mesh, in_specs=in_specs, out_specs=out_specs, check_vma=False)
```

profile of v0, /device:TPU:1, one launch (start us, length us, event | category | flops | bytes accessed | tf_op | source)
XLA Modules:
  0.0 333.1 jit_solution(12433743800560225065)
XLA Ops:
  7.3 1.0 dynamic-slice_reduce_fusion
  8.3 0.8 compare_convert_fusion
  9.0 1.2 reduce-window.6
  10.6 0.8 fusion.41
  11.4 3.1 scatter_custom_fusion
  14.6 0.3 constant_dynamic-slice_fusion
  15.0 0.3 reshape.96
  15.4 0.1 copy.82
  15.7 1.8 convolution_convert_fusion
  17.6 81.6 %all_to_all.10 = bf16[32,32,3072]{2,1,0:T(8,128)(2,1)} all-to-all(bf16[32,32,3072]{2,1,0:T(8,128)(2,1)S(1)} %bitcast.60), channel_id=1, replica_groups=mesh['dp'=8,'own'=32] {'own'}, dimensions={0} | all-to-all | bytes 12582912 | tf_op jit(solution)/shard_map/all_to_all | solution.py:167
  99.1 12.4 %reshape.98 = bf16[32,32,2,12,128]{4,3,2,1,0:T(8,128)(2,1)} reshape(bf16[32,32,3072]{2,1,0:T(8,128)(2,1)} %all_to_all.10) | data formatting | bytes 12582912 | tf_op jit(solution)/shard_map/reshape | solution.py:168
  111.5 7.4 %copy.85 = bf16[32,2,32,12,128]{4,0,3,2,1:T(8,128)(2,1)S(1)} copy(bf16[32,2,32,12,128]{4,3,1,0,2:T(8,128)(2,1)} %bitcast.61) | data formatting | bytes 12582912 | tf_op jit(solution)/shard_map/transpose | solution.py:169
  118.9 2.7 fusion.50
  121.7 5.3 %fusion = f32[32,128,128]{2,1,0:T(8,128)S(1)} fusion(bf16[32,1,384,128]{3,0,2,1:T(8,128)(2,1)} %get-tuple-element.37, bf16[32,128,768]{2,1,0:T(8,128)(2,1)} %all-gather.4.cloned.1.call-done), kind=kOutput, calls=%fused_computation.6 | convolution fusion | flops 402653184 | bytes 8388608 | tf_op jit(solution)/shard_map/kcs,ksw->kcw/dot_general | solution.py:172
  127.0 1.3 copy-done.3
  128.3 6.0 %fusion.2 = f32[32,128,384]{2,1,0:T(8,128)} fusion(bf16[32,1,384,128]{3,0,2,1:T(8,128)(2,1)S(1)} %get-tuple-element.38, f32[32,128,128]{2,1,0:T(8,128)S(1)} %fusion), kind=kOutput, calls=%fused_computation.12 | convolution fusion | flops 407371776 | bytes 11534336 | tf_op jit(solution)/shard_map/kcw,ksw->kcs/dot_general | solution.py:175
  134.4 10.8 %convert_bitcast_fusion.1 = bf16[32,1,384,128]{3,2,0,1:T(8,128)(2,1)} fusion(bf16[32,128,768]{2,1,0:T(8,128)(2,1)} %all-gather.4.cloned.1.call-done, f32[32,128,128]{2,1,0:T(8,128)} %copy-done.3, bf16[32,1,384,128]{3,0,2,1:T(8,128)(2,1)S(1)} %get-tuple-element.38), kind=kOutput, calls=%fused_computation.8 | convolution fusion | flops 816840704 | bytes 14680064 | tf_op jit(solution)/shard_map/kcs,kcw->ksw/dot_general | solution.py:180
  145.2 4.2 %convert_bitcast_fusion = bf16[32,1,384,128]{3,2,0,1:T(8,128)(2,1)S(1)} fusion(bf16[32,128,768]{2,1,0:T(8,128)(2,1)} %all-gather.4.cloned.1.call-done, f32[32,128,128]{2,1,0:T(8,128)} %copy-done.3), kind=kOutput, calls=%fused_computation.7 | convolution fusion | flops 408944640 | bytes 8388608 | tf_op jit(solution)/shard_map/kcs,kcw->ksw/dot_general | solution.py:181
  149.5 3.2 pad_maximum_fusion
  152.7 0.2 all-gather.6.cloned.1.call-start
  152.9 6.8 %copy.90 = bf16[32,2,384,128]{3,0,2,1:T(8,128)(2,1)S(1)} copy(bf16[32,2,384,128]{3,2,0,1:T(8,128)(2,1)} %pad_maximum_fusion) | data formatting | bytes 12582912 | tf_op jit(solution)/shard_map/optimization_barrier | solution.py:183
  159.7 6.3 %copy.91 = bf16[32,32,2,12,128]{4,3,2,1,0:T(8,128)(2,1)} copy(bf16[32,32,2,12,128]{4,1,3,0,2:T(8,128)(2,1)S(1)} %bitcast.65) | data formatting | bytes 12582912 | tf_op jit(solution)/shard_map/transpose | solution.py:185
  166.0 12.1 %reshape.101 = bf16[32,32,3072]{2,1,0:T(8,128)(2,1)} reshape(bf16[32,32,2,12,128]{4,3,2,1,0:T(8,128)(2,1)} %copy.91) | data formatting | bytes 12582912 | tf_op jit(solution)/shard_map/reshape | solution.py:186
  178.1 78.2 %all_to_all.11 = bf16[32,32,3072]{2,1,0:T(8,128)(2,1)} all-to-all(bf16[32,32,3072]{2,1,0:T(8,128)(2,1)} %reshape.101), channel_id=1, replica_groups=mesh['dp'=8,'own'=32] {'own'}, dimensions={0} | all-to-all | bytes 12582912 | tf_op jit(solution)/shard_map/all_to_all | solution.py:187
  256.3 8.7 %copy.93 = bf16[3072,1024]{1,0:T(8,128)(2,1)} copy(bf16[3072,1024]{0,1:T(8,128)(2,1)} %bitcast.63) | data formatting | bytes 12582912 | tf_op jit(solution)/shard_map/dot_general | solution.py:129
  265.1 6.1 %subtract_convert_fusion = (bf16[64,2,12,128]{3,0,2,1:T(8,128)(2,1)}, f32[64,2,12,128]{3,0,2,1:T(8,128)S(1)}, f32[64,2,12,128]{3,0,2,1:T(8,128)S(1)}) fusion(bf16[64,2,12,128]{3,1,2,0:T(2,128)(2,1)S(1)} %constant_dynamic-slice_fusion, f32[64,2,12,128]{3,1,2,0:T(2,128)S(1)} %copy-done.4, f32[64,2,12,128]{3,1,2,0:T(2,128)S(1)} %copy-done.5, ...), kind=kOutput, calls=%fused_computation.37 | convolution fusion | flops 405471232 | bytes 10227712 | tf_op jit(solution)/shard_map/dot_general | solution.py:129
  271.2 1.5 copy.96
  272.7 1.5 copy.97
  274.3 1.8 gather_fusion
  276.1 39.0 %all-gather.6.cloned.1.call-done = bf16[512,2,12,128]{3,0,2,1:T(8,128)(2,1)} async-done(((bf16[64,2,12,128]{3,0,2,1:T(8,128)(2,1)}), bf16[512,2,12,128]{3,0,2,1:T(8,128)(2,1)}) %all-gather.6.cloned.1.call-update) | async-done | bytes 3145744 | tf_op jit(solution)/shard_map/all_gather | solution.py:195
  315.1 5.8 %copy.95 = bf16[64,2,12,8,128]{4,3,1,2,0:T(8,128)(2,1)} copy(bf16[64,2,12,8,128]{4,0,3,2,1:T(8,128)(2,1)} %bitcast.67) | data formatting | bytes 6291456 | tf_op jit(solution)/shard_map/transpose | solution.py:196
  320.9 5.5 %reshape.104 = bf16[64,2,12,1024]{3,1,2,0:T(2,128)(2,1)} reshape(bf16[64,2,12,8,128]{4,3,1,2,0:T(8,128)(2,1)} %copy.95) | data formatting | bytes 6291456 | tf_op jit(solution)/shard_map/reshape | solution.py:196
  (38 shorter events, 1.0 us)
Async XLA Ops:
  7.2 7.4 %copy-start = (bf16[64,2,12,1024]{3,1,2,0:T(2,128)(2,1)S(1)}, bf16[64,2,12,1024]{3,1,2,0:T(2,128)(2,1)}, u32[]{:S(2)}) copy-start(bf16[64,2,12,1024]{3,1,2,0:T(2,128)(2,1)} %param.13) | copy-start | bytes 9437188
  7.2 8.1 %copy-start.7 = (s32[256,4]{0,1:T(4,128)S(1)}, s32[256,4]{0,1:T(4,128)}, u32[]{:S(2)}) copy-start(s32[256,4]{0,1:T(4,128)} %param.11) | copy-start | bytes 12292
  7.2 8.1 %copy-start.8 = (s32[64]{0:T(128)S(1)}, s32[64]{0:T(128)}, u32[]{:S(2)}) copy-start(s32[64]{0:T(128)} %param.12) | copy-start | bytes 772
  7.2 114.5 %all-gather.4.cloned.1.call-start = ((), (), s32[]{:S(2)}) async-start(), calls=%async_computation.3 | async-start | bytes 7077888 | tf_op jit(solution)/shard_map/all_gather | solution.py:157
  14.5 241.8 %reduce-scatter.2.cloned.1.call-start = ((), (), s32[]{:S(2)}) async-start(), calls=%async_computation.4 | async-start | bytes 7077888 | tf_op jit(solution)/shard_map/reduce_scatter | solution.py:184
  127.0 1.4 copy-start.3
  145.2 4.2 %copy-start.2 = (bf16[32,1,384,128]{3,2,0,1:T(8,128)(2,1)S(1)}, bf16[32,1,384,128]{3,2,0,1:T(8,128)(2,1)}, u32[]{:S(2)}) copy-start(bf16[32,1,384,128]{3,2,0,1:T(8,128)(2,1)} %convert_bitcast_fusion.1) | copy-start | bytes 9437188
  152.7 162.4 %all-gather.6.cloned.1.call-start = ((), (), s32[]{:S(2)}) async-start(), calls=%async_computation.5 | async-start | bytes 3538944 | tf_op jit(solution)/shard_map/all_gather | solution.py:195
  256.3 8.8 %copy-start.4 = (f32[64,2,12,128]{3,1,2,0:T(2,128)S(1)}, f32[64,2,12,128]{3,1,2,0:T(2,128)}, u32[]{:S(2)}) copy-start(f32[64,2,12,128]{3,1,2,0:T(2,128)} %param.14) | copy-start | bytes 2359300
  256.3 8.8 %copy-start.5 = (f32[64,2,12,128]{3,1,2,0:T(2,128)S(1)}, f32[64,2,12,128]{3,1,2,0:T(2,128)}, u32[]{:S(2)}) copy-start(f32[64,2,12,128]{3,1,2,0:T(2,128)} %param.15) | copy-start | bytes 2359300
  271.2 3.0 copy-start.6
  315.1 11.3 %copy-start.1 = (bf16[64,2,12,1024]{3,1,2,0:T(2,128)(2,1)S(1)}, bf16[64,2,12,1024]{3,1,2,0:T(2,128)(2,1)}, u32[]{:S(2)}) copy-start(bf16[64,2,12,1024]{3,1,2,0:T(2,128)(2,1)} %param.13) | copy-start | bytes 9437188
Sparse Core Ops, SparseCore 0:
  14.6 78.2 all-gather.3
  152.8 74.2 reduce-scatter.1
  271.3 43.7 all-gather.5
where the time goes:
time: 339 us; the launch traced here: 333 us
  blocking collectives  160 us (47%)
  local copies, waits for them, and re-layouts  76.2 us (22%)
  waiting for transfers between devices  39.1 us (12%)
  matrix products  34.4 us (10%)
  between operations  14.1 us (4%)
  other arithmetic  9.27 us (3%)
    all_to_all x1, blocking collectives, shards(): lax.all_to_all(outgoing, 'own', split_axis=0, concat_axis=0, tiled=True)  81.6 us
    all_to_all x1, blocking collectives, shards(): lax.all_to_all(pieces, 'own', split_axis=0, concat_axis=0, tiled=True)  78.2 us
    all_gather x1, waiting for transfers between devices, shards(): new_weights = lax.all_gather(fresh_part, 'dp', axis=0, tiled=False)  39 us
    reshape x1, local copies, waits for them, and re-layouts, shards(): arrived = arrived.reshape(n_own, pairs, 2, piece_rows, width_part)  12.4 us
    reshape x1, local copies, waits for them, and re-layouts, shards(): pieces = pieces.reshape(n_own, pairs, 2 * piece_rows * width_part)  12.1 us
    dot_general x1, matrix products, shards(): jnp.einsum('kcs,kcw->ksw', sig_slots, back_pre, preferred_element_type=jn...  10.8 us
    dot_general x1, local copies, waits for them, and re-layouts, sum_by_insertion(): return jnp.dot(one_hot, flat_grad, preferred_element_type=jnp.float32)  8.75 us
    transpose x1, local copies, waits for them, and re-layouts, shards(): arrived.transpose(1, 2, 0, 3, 4).reshape(pairs, 2, SITES, width_part)  7.43 us
  transfers between devices with their start and end apart: 3, of which 1 were waited for; matrix products, arithmetic and copies ran while one was open for 17% of the time, Pallas kernels for 0%

commit v1 on v0

--- a/solution.py
+++ b/solution.py
@@ -164,32 +164,60 @@
         pick, my_width.reshape(number, -1), preferred_element_type=jnp.float32
     ).astype(weights.dtype)
     outgoing = outgoing.reshape(n_own, pairs, 2 * piece_rows * width_part)
-    arrived = lax.all_to_all(outgoing, "own", split_axis=0, concat_axis=0, tiled=True)
-    arrived = arrived.reshape(n_own, pairs, 2, piece_rows, width_part)
-    arrived = arrived.transpose(1, 2, 0, 3, 4).reshape(pairs, 2, SITES, width_part)
-    read_in = arrived[:, 0]
-    read_out = arrived[:, 1]
-    preact = jnp.einsum("kcs,ksw->kcw", sig_slots, read_in, preferred_element_type=jnp.float32)
-    gelu_val, slopes = gelu_parts(preact)
-    hidden = gelu_val.astype(jnp.bfloat16)
-    pred_part = jnp.einsum("kcw,ksw->kcs", hidden, read_out, preferred_element_type=jnp.float32)
-    back_hidden = jnp.einsum(
-        "kcs,ksw->kcw", cot_slots, read_out, preferred_element_type=jnp.float32
-    )
-    back_pre = (back_hidden * slopes).astype(jnp.bfloat16)
-    grad_in = jnp.einsum("kcs,kcw->ksw", sig_slots, back_pre, preferred_element_type=jnp.float32)
-    grad_out = jnp.einsum("kcs,kcw->ksw", cot_slots, hidden, preferred_element_type=jnp.float32)
-    grads = jnp.stack([grad_in, grad_out], axis=1).astype(jnp.bfloat16)
-    pred_part, grads = lax.optimization_barrier((pred_part, grads))
-    pred_slots = lax.psum_scatter(pred_part, "dp", scatter_dimension=0, tiled=True)
-    pieces = grads.reshape(pairs, 2, n_own, piece_rows, width_part).transpose(2, 0, 1, 3, 4)
-    pieces = pieces.reshape(n_own, pairs, 2 * piece_rows * width_part)
-    arrived_grad = lax.all_to_all(pieces, "own", split_axis=0, concat_axis=0, tiled=True)
-    arrived_grad, pred_slots = lax.optimization_barrier((arrived_grad, pred_slots))
+    item_rows = peer_rows.reshape(n_own, pairs)
+    halves = 2
+    half = pairs // halves
+    pred_parts = []
+    table = None
+    fetched = [
+        lax.all_to_all(
+            outgoing[:, h * half : (h + 1) * half], "own", split_axis=0, concat_axis=0, tiled=True
+        )
+        for h in range(halves)
+    ]
+    sent = None
+    for h in range(halves):
+        chosen = slice(h * half, (h + 1) * half)
+        arrived = fetched[h]
+        arrived = arrived.reshape(n_own, half, 2, piece_rows, width_part)
+        arrived = arrived.transpose(1, 2, 0, 3, 4).reshape(half, 2, SITES, width_part)
+        read_in = arrived[:, 0]
+        read_out = arrived[:, 1]
+        sig_part = sig_slots[chosen]
+        cot_part = cot_slots[chosen]
+        preact = jnp.einsum("kcs,ksw->kcw", sig_part, read_in, preferred_element_type=jnp.float32)
+        gelu_val, slopes = gelu_parts(preact)
+        hidden = gelu_val.astype(jnp.bfloat16)
+        pred_parts.append(
+            jnp.einsum("kcw,ksw->kcs", hidden, read_out, preferred_element_type=jnp.float32)
+        )
+        back_hidden = jnp.einsum(
+            "kcs,ksw->kcw", cot_part, read_out, preferred_element_type=jnp.float32
+        )
+        back_pre = (back_hidden * slopes).astype(jnp.bfloat16)
+        grad_in = jnp.einsum("kcs,kcw->ksw", sig_part, back_pre, preferred_element_type=jnp.float32)
+        grad_out = jnp.einsum("kcs,kcw->ksw", cot_part, hidden, preferred_element_type=jnp.float32)
+        grads = jnp.stack([grad_in, grad_out], axis=1).astype(jnp.bfloat16)
+        if h + 1 < halves:
+            grads, fetched[h + 1] = lax.optimization_barrier((grads, fetched[h + 1]))
+        if sent is not None:
+            grads, sent = lax.optimization_barrier((grads, sent))
+            table = sum_by_insertion(item_rows[:, :half].reshape(-1), sent, number)
+        if h == halves - 1:
+            pred_part = jnp.concatenate(pred_parts, axis=0)
+            pred_part, grads = lax.optimization_barrier((pred_part, grads))
+            pred_slots = lax.psum_scatter(pred_part, "dp", scatter_dimension=0, tiled=True)
+        pieces = grads.reshape(half, 2, n_own, piece_rows, width_part).transpose(2, 0, 1, 3, 4)
+        pieces = pieces.reshape(n_own, half, 2 * piece_rows * width_part)
+        arrived_grad = lax.all_to_all(pieces, "own", split_axis=0, concat_axis=0, tiled=True)
+        if h == halves - 1:
+            arrived_grad, pred_slots = lax.optimization_barrier((arrived_grad, pred_slots))
+            part = sum_by_insertion(item_rows[:, chosen].reshape(-1), arrived_grad, number)
+            table = part + table
+        else:
+            sent = arrived_grad
     pred_slots = pred_slots.astype(jnp.bfloat16)
-    table = sum_by_insertion(peer_rows, arrived_grad, number).reshape(
-        number, 2, piece_rows, width_part
-    )
+    table = table.reshape(number, 2, piece_rows, width_part)
     own_params = my_width.astype(jnp.float32)
     fresh_part, new_moment1, new_moment2 = adam_step(own_params, moment1, moment2, table)
     new_weights = lax.all_gather(fresh_part, "dp", axis=0, tiled=False)

time: 339 us -> 316 us (0.932)
  blocking collectives: 160 us -> 47.9 us
  waiting for transfers between devices: 39.1 us -> 111 us
  starting transfers between devices: 0.29 us -> 15 us
  other arithmetic: 9.27 us -> 18.9 us
  matrix products: 34.4 us -> 29.3 us
    all_to_all x2 -> x1, blocking collectives: 160 us -> 47.9 us  [shards(): lax.all_to_all(outgoing[:, h * half:(h + 1) * half], 'own', split_axis=0,...]
    all_to_all x0 -> x3, waiting for transfers between devices: none -> 48.1 us  [the longest x2 46 us: shards(): lax.all_to_all(pieces, 'own', split_axis=0, concat_axis=0, tiled=True)]
    reduce_scatter x1, waiting for transfers between devices: 0.01 us -> 16.2 us  [shards(): lax.psum_scatter(pred_part, 'dp', scatter_dimension=0, tiled=True)]
    all_to_all x0 -> x3, starting transfers between devices: none -> 14.9 us  [the longest x2 10.3 us: shards(): lax.all_to_all(pieces, 'own', split_axis=0, concat_axis=0, tiled=True)]
    dot_general x1 -> x0, local copies, waits for them, and re-layouts: 8.75 us -> none  [sum_by_insertion(): return jnp.dot(one_hot, flat_grad, preferred_element_type=jnp.float32)]
    all_gather x1, waiting for transfers between devices: 0.01 us -> 7.57 us  [shards(): lax.all_gather(stacked.reshape(TOUCH, CAP, 2 * SITES), 'dp', axis=0, tile...]
    slice x2 -> x7, local copies, waits for them, and re-layouts: 0.18 us -> 6.72 us  [the longest x1 2.24 us: shards(): read_out = arrived[:, 1]]
    transpose x3 -> x4, local copies, waits for them, and re-layouts: 19.5 us -> 14.7 us  [the longest x2 8.44 us: shards(): arrived.transpose(1, 2, 0, 3, 4).reshape(half, 2, SITES, width_part)]
  transfers between devices with their start and end apart: 3 -> 6, of which waited for: 1 -> 6; matrix products, arithmetic and copies ran while one was open for 17% -> 27% of each run, Pallas kernels for 0% -> 0%
where the time goes in v1:
time: 316 us; the launch traced here: 311 us
  waiting for transfers between devices  111 us (35%)
  local copies, waits for them, and re-layouts  74.3 us (24%)
  blocking collectives  47.9 us (15%)
  matrix products  29.3 us (9%)
  other arithmetic  18.9 us (6%)
  starting transfers between devices  15 us (5%)
  between operations  14.3 us (5%)
    all_to_all x1, blocking collectives, shards(): lax.all_to_all(outgoing[:, h * half:(h + 1) * half], 'own', split_axis=0,...  47.9 us
    all_to_all x2, waiting for transfers between devices, shards(): lax.all_to_all(pieces, 'own', split_axis=0, concat_axis=0, tiled=True)  46 us
    all_gather x1, waiting for transfers between devices, shards(): new_weights = lax.all_gather(fresh_part, 'dp', axis=0, tiled=False)  39 us
    reduce_scatter x1, waiting for transfers between devices, shards(): lax.psum_scatter(pred_part, 'dp', scatter_dimension=0, tiled=True)  16.2 us
    reshape x2, local copies, waits for them, and re-layouts, shards(): pieces = pieces.reshape(n_own, half, 2 * piece_rows * width_part)  13.8 us
    dot_general x2, matrix products, shards(): jnp.einsum('kcs,kcw->ksw', sig_part, back_pre, preferred_element_type=jnp...  11.1 us
    reshape x2, local copies, waits for them, and re-layouts, shards(): arrived = arrived.reshape(n_own, half, 2, piece_rows, width_part)  10.6 us
    all_to_all x2, starting transfers between devices, shards(): lax.all_to_all(pieces, 'own', split_axis=0, concat_axis=0, tiled=True)  10.3 us
  transfers between devices with their start and end apart: 6, of which 6 were waited for; matrix products, arithmetic and copies ran while one was open for 27% of the time, Pallas kernels for 0%

profile of v1, /device:TPU:1, one launch (start us, length us, event | category | flops | bytes accessed | tf_op | source)
XLA Modules:
  0.0 310.6 jit_solution(8814415489096847361)
XLA Ops:
  11.4 3.1 scatter_custom_fusion
  19.7 47.9 %all_to_all.20 = bf16[32,16,3072]{2,1,0:T(8,128)(2,1)} all-to-all(bf16[32,16,3072]{2,1,0:T(8,128)(2,1)S(1)} %get-tuple-element.42), channel_id=1, replica_groups=mesh['dp'=8,'own'=32] {'own'}, dimensions={0} | all-to-all | bytes 6291456 | tf_op jit(solution)/shard_map/all_to_all | solution.py:173
  67.6 4.5 %all-to-all-start.1 = ((bf16[32,16,3072]{2,1,0:T(8,128)(2,1)}), bf16[32,16,3072]{2,1,0:T(8,128)(2,1)S(1)}, u32[]{:S(2)}, u32[]{:S(2)}) async-start(bf16[32,16,3072]{2,1,0:T(8,128)(2,1)} %get-tuple-element.41), calls=%async_computation.1 | async-start | bytes 6291456 | tf_op jit(solution)/shard_map/all_to_all | solution.py:173
  72.1 6.8 %reshape.115 = bf16[32,16,2,12,128]{4,3,2,1,0:T(8,128)(2,1)} reshape(bf16[32,16,3072]{2,1,0:T(8,128)(2,1)} %all_to_all.20) | data formatting | bytes 6291456 | tf_op jit(solution)/shard_map/reshape | solution.py:182
  78.9 4.2 %copy.110 = bf16[16,2,32,12,128]{4,0,3,2,1:T(8,128)(2,1)S(1)} copy(bf16[16,2,32,12,128]{4,3,1,0,2:T(8,128)(2,1)} %bitcast.78) | data formatting | bytes 6291456 | tf_op jit(solution)/shard_map/transpose | solution.py:183
  83.1 2.2 fusion.83
  85.4 7.6 %all-gather.4.cloned.1.call-done = bf16[32,128,768]{2,1,0:T(8,128)(2,1)} async-done(((bf16[4,128,768]{2,1,0:T(8,128)(2,1)}), bf16[32,128,768]{2,1,0:T(8,128)(2,1)}) %all-gather.4.cloned.1.call-update) | async-done | bytes 6291472 | tf_op jit(solution)/shard_map/all_gather | solution.py:157
  92.9 2.7 fusion.1
  96.6 3.4 %fusion.3 = bf16[16,1,384,128]{3,2,0,1:T(8,128)(2,1)} fusion(bf16[32,128,768]{2,1,0:T(8,128)(2,1)} %all-gather.4.cloned.1.call-done, f32[16,128,128]{2,1,0:T(8,128)S(1)} %fusion.1), kind=kOutput, calls=%fused_computation.24 | convolution fusion | flops 204472320 | bytes 4194304 | tf_op jit(solution)/shard_map/kcs,kcw->ksw/dot_general | solution.py:199
  100.0 5.7 %fusion.2 = bf16[16,1,384,128]{3,2,0,1:T(8,128)(2,1)} fusion(bf16[32,128,768]{2,1,0:T(8,128)(2,1)} %all-gather.4.cloned.1.call-done, bf16[16,1,384,128]{3,0,2,1:T(8,128)(2,1)} %get-tuple-element.45, f32[16,128,128]{2,1,0:T(8,128)} %copy-done.5), kind=kOutput, calls=%fused_computation.23 | convolution fusion | flops 408420352 | bytes 7340032 | tf_op jit(solution)/shard_map/kcs,kcw->ksw/dot_general | solution.py:198
  105.8 3.9 %pad_maximum_fusion.1 = bf16[16,2,384,128]{3,2,0,1:T(8,128)(2,1)} fusion(bf16[16,1,384,128]{3,2,0,1:T(8,128)(2,1)} %fusion.3, bf16[16,1,384,128]{3,2,0,1:T(8,128)(2,1)} %fusion.2), kind=kLoop, calls=%fused_computation.6 | loop fusion | flops 1572864 | bytes 6291456 | tf_op jit(solution)/shard_map/stack | solution.py:200
  111.8 3.9 %copy.120 = bf16[16,2,384,128]{3,0,2,1:T(8,128)(2,1)S(1)} copy(bf16[16,2,384,128]{3,2,0,1:T(8,128)(2,1)} %pad_maximum_fusion.1) | data formatting | bytes 6291456 | tf_op jit(solution)/shard_map/optimization_barrier | solution.py:202
  115.7 3.1 %copy.121 = bf16[32,16,2,12,128]{4,3,2,1,0:T(8,128)(2,1)} copy(bf16[32,16,2,12,128]{4,1,3,0,2:T(8,128)(2,1)S(1)} %bitcast.82) | data formatting | bytes 6291456 | tf_op jit(solution)/shard_map/transpose | solution.py:210
  118.8 6.7 %reshape.120 = bf16[32,16,3072]{2,1,0:T(8,128)(2,1)} reshape(bf16[32,16,2,12,128]{4,3,2,1,0:T(8,128)(2,1)} %copy.121) | data formatting | bytes 6291456 | tf_op jit(solution)/shard_map/reshape | solution.py:211
  125.5 5.5 %all-to-all-start.2 = ((bf16[32,16,3072]{2,1,0:T(8,128)(2,1)}), bf16[32,16,3072]{2,1,0:T(8,128)(2,1)}, u32[]{:S(2)}, u32[]{:S(2)}) async-start(bf16[32,16,3072]{2,1,0:T(8,128)(2,1)} %reshape.120), calls=%async_computation.2 | async-start | bytes 6291456 | tf_op jit(solution)/shard_map/all_to_all | solution.py:212
  131.1 3.8 %reshape.117 = bf16[32,16,2,12,128]{4,3,2,1,0:T(8,128)(2,1)} reshape(bf16[32,16,3072]{2,1,0:T(8,128)(2,1)S(1)} %all-to-all-done.1) | data formatting | bytes 6291456 | tf_op jit(solution)/shard_map/reshape | solution.py:182
  134.9 4.2 %copy.115 = bf16[16,2,32,12,128]{4,0,3,2,1:T(8,128)(2,1)S(1)} copy(bf16[16,2,32,12,128]{4,3,1,0,2:T(8,128)(2,1)} %bitcast.79) | data formatting | bytes 6291456 | tf_op jit(solution)/shard_map/transpose | solution.py:183
  140.8 2.2 fusion
  143.9 2.4 fusion.5
  146.4 5.3 %fusion.4 = bf16[16,1,384,128]{3,2,0,1:T(8,128)(2,1)} fusion(bf16[32,128,768]{2,1,0:T(8,128)(2,1)} %all-gather.4.cloned.1.call-done, bf16[16,1,384,128]{3,0,2,1:T(8,128)(2,1)S(1)} %copy-done.3, f32[16,128,128]{2,1,0:T(8,128)} %copy-done.7), kind=kOutput, calls=%fused_computation.25 | convolution fusion | flops 408420352 | bytes 7340032 | tf_op jit(solution)/shard_map/kcs,kcw->ksw/dot_general | solution.py:198
  151.7 3.5 %pad_maximum_fusion.2 = bf16[16,2,384,128]{3,2,0,1:T(8,128)(2,1)} fusion(bf16[16,1,384,128]{3,2,0,1:T(8,128)(2,1)S(1)} %fusion.5, bf16[16,1,384,128]{3,2,0,1:T(8,128)(2,1)} %fusion.4), kind=kLoop, calls=%fused_computation.7 | loop fusion | flops 1572864 | bytes 6291456 | tf_op jit(solution)/shard_map/stack | solution.py:200
  157.8 3.2 %pad_maximum_fusion = f32[32,128,384]{2,1,0:T(8,128)} fusion(f32[16,128,384]{2,1,0:T(8,128)S(1)} %fusion.9, f32[16,128,384]{2,1,0:T(8,128)S(1)} %fusion.7), kind=kLoop, calls=%fused_computation.2 | loop fusion | flops 1572864 | bytes 12582912 | tf_op jit(solution)/shard_map/concatenate | solution.py:207
  161.1 9.8 %all-to-all-done.2 = bf16[32,16,3072]{2,1,0:T(8,128)(2,1)} async-done(((bf16[32,16,3072]{2,1,0:T(8,128)(2,1)}), bf16[32,16,3072]{2,1,0:T(8,128)(2,1)}, u32[]{:S(2)}, u32[]{:S(2)}) %all-to-all-start.2) | async-done | bytes 3145760 | tf_op jit(solution)/shard_map/all_to_all | solution.py:212
  170.9 3.9 %copy.122 = bf16[16,2,384,128]{3,0,2,1:T(8,128)(2,1)S(1)} copy(bf16[16,2,384,128]{3,2,0,1:T(8,128)(2,1)} %pad_maximum_fusion.2) | data formatting | bytes 6291456 | tf_op jit(solution)/shard_map/optimization_barrier | solution.py:208
  174.8 3.1 %copy.123 = bf16[32,16,2,12,128]{4,3,2,1,0:T(8,128)(2,1)} copy(bf16[32,16,2,12,128]{4,1,3,0,2:T(8,128)(2,1)S(1)} %bitcast.83) | data formatting | bytes 6291456 | tf_op jit(solution)/shard_map/transpose | solution.py:210
  177.9 7.1 %reshape.122 = bf16[32,16,3072]{2,1,0:T(8,128)(2,1)} reshape(bf16[32,16,2,12,128]{4,3,2,1,0:T(8,128)(2,1)} %copy.123) | data formatting | bytes 6291456 | tf_op jit(solution)/shard_map/reshape | solution.py:211
  185.0 4.9 %all-to-all-start.3 = ((bf16[32,16,3072]{2,1,0:T(8,128)(2,1)}), bf16[32,16,3072]{2,1,0:T(8,128)(2,1)S(1)}, u32[]{:S(2)}, u32[]{:S(2)}) async-start(bf16[32,16,3072]{2,1,0:T(8,128)(2,1)} %reshape.122), calls=%async_computation.3 | async-start | bytes 6291456 | tf_op jit(solution)/shard_map/all_to_all | solution.py:212
  193.4 36.2 %all-to-all-done.3 = bf16[32,16,3072]{2,1,0:T(8,128)(2,1)S(1)} async-done(((bf16[32,16,3072]{2,1,0:T(8,128)(2,1)}), bf16[32,16,3072]{2,1,0:T(8,128)(2,1)S(1)}, u32[]{:S(2)}, u32[]{:S(2)}) %all-to-all-start.3) | async-done | bytes 3145760 | tf_op jit(solution)/shard_map/all_to_all | solution.py:212
  229.6 16.2 %reduce-scatter.2.cloned.1.call-done = f32[4,128,384]{2,1,0:T(8,128)} async-done(((f32[32,128,384]{2,1,0:T(8,128)}), f32[4,128,384]{2,1,0:T(8,128)}) %reduce-scatter.2.cloned.1.call-update) | async-done | bytes 786448 | tf_op jit(solution)/shard_map/reduce_scatter | solution.py:209
  247.2 2.5 convolution_add_fusion
  257.6 39.0 %all-gather.6.cloned.1.call-done = bf16[512,2,12,128]{3,1,2,0:T(2,128)(2,1)} async-done(((bf16[64,2,12,128]{3,1,2,0:T(2,128)(2,1)}), bf16[512,2,12,128]{3,1,2,0:T(2,128)(2,1)}) %all-gather.6.cloned.1.call-update) | async-done | bytes 3145744 | tf_op jit(solution)/shard_map/all_gather | solution.py:223
  296.7 7.2 %copy.177 = bf16[8,64,12,1,2,128]{5,4,0,3,2,1:T(2,128)(2,1)} copy(bf16[8,64,12,1,2,128]{5,4,3,2,1,0:T(2,128)(2,1)} %bitcast.86) | data formatting | bytes 6291456 | tf_op jit(solution)/shard_map/reshape | solution.py:224
  (76 shorter events, 30.5 us)
Async XLA Ops:
  7.2 7.4 %copy-start = (bf16[64,2,12,1024]{3,1,2,0:T(2,128)(2,1)S(1)}, bf16[64,2,12,1024]{3,1,2,0:T(2,128)(2,1)}, u32[]{:S(2)}) copy-start(bf16[64,2,12,1024]{3,1,2,0:T(2,128)(2,1)} %param.13) | copy-start | bytes 9437188
  7.2 8.0 %copy-start.10 = (s32[256,4]{0,1:T(4,128)S(1)}, s32[256,4]{0,1:T(4,128)}, u32[]{:S(2)}) copy-start(s32[256,4]{0,1:T(4,128)} %param.11) | copy-start | bytes 12292
  7.2 8.0 %copy-start.14 = (s32[64]{0:T(128)S(1)}, s32[64]{0:T(128)}, u32[]{:S(2)}) copy-start(s32[64]{0:T(128)} %param.12) | copy-start | bytes 772
  7.2 85.7 %all-gather.4.cloned.1.call-start = ((), (), s32[]{:S(2)}) async-start(), calls=%async_computation.5 | async-start | bytes 7077888 | tf_op jit(solution)/shard_map/all_gather | solution.py:157
  11.4 3.1 copy-start.12
  67.6 44.2 %all-to-all-start.1 = ((bf16[32,16,3072]{2,1,0:T(8,128)(2,1)}), bf16[32,16,3072]{2,1,0:T(8,128)(2,1)S(1)}, u32[]{:S(2)}, u32[]{:S(2)}) async-start(bf16[32,16,3072]{2,1,0:T(8,128)(2,1)} %get-tuple-element.41), calls=%async_computation.1 | async-start | bytes 6291456 | tf_op jit(solution)/shard_map/all_to_all | solution.py:173
  95.6 1.0 copy-start.5
  125.5 45.3 %all-to-all-start.2 = ((bf16[32,16,3072]{2,1,0:T(8,128)(2,1)}), bf16[32,16,3072]{2,1,0:T(8,128)(2,1)}, u32[]{:S(2)}, u32[]{:S(2)}) async-start(bf16[32,16,3072]{2,1,0:T(8,128)(2,1)} %reshape.120), calls=%async_computation.2 | async-start | bytes 6291456 | tf_op jit(solution)/shard_map/all_to_all | solution.py:212
  131.0 114.8 %reduce-scatter.2.cloned.1.call-start = ((), (), s32[]{:S(2)}) async-start(), calls=%async_computation.6 | async-start | bytes 7077888 | tf_op jit(solution)/shard_map/reduce_scatter | solution.py:209
  143.0 1.0 copy-start.7
  143.9 2.4 copy-start.3
  151.7 3.5 %copy-start.4 = (bf16[16,1,384,128]{3,0,2,1:T(8,128)(2,1)S(1)}, bf16[16,1,384,128]{3,0,2,1:T(8,128)(2,1)}, u32[]{:S(2)}) copy-start(bf16[16,1,384,128]{3,0,2,1:T(8,128)(2,1)} %get-tuple-element.44) | copy-start | bytes 4718596
  151.7 3.5 %copy-start.8 = (f32[16,128,128]{2,1,0:T(8,128)S(1)}, f32[16,128,128]{2,1,0:T(8,128)}, u32[]{:S(2)}) copy-start(f32[16,128,128]{2,1,0:T(8,128)} %copy-done.7) | copy-start | bytes 3145732
  155.2 1.4 copy-start.2
  155.2 1.7 copy-start.6
  185.0 44.6 %all-to-all-start.3 = ((bf16[32,16,3072]{2,1,0:T(8,128)(2,1)}), bf16[32,16,3072]{2,1,0:T(8,128)(2,1)S(1)}, u32[]{:S(2)}, u32[]{:S(2)}) async-start(bf16[32,16,3072]{2,1,0:T(8,128)(2,1)} %reshape.122), calls=%async_computation.3 | async-start | bytes 6291456 | tf_op jit(solution)/shard_map/all_to_all | solution.py:212
  189.9 106.8 %all-gather.6.cloned.1.call-start = ((), (), s32[]{:S(2)}) async-start(), calls=%async_computation.7 | async-start | bytes 3538944 | tf_op jit(solution)/shard_map/all_gather | solution.py:223
  193.4 53.7 %copy-start.11 = (s32[512]{0:T(512)S(1)}, s32[512]{0:T(512)}, u32[]{:S(2)}) copy-start(s32[512]{0:T(512)} %eq.103) | copy-start | bytes 6148
  249.9 3.2 %copy-start.13 = (s32[256,1]{0,1:T(1,128)S(1)}, s32[256,1]{0,1:T(1,128)}, u32[]{:S(2)}) copy-start(s32[256,1]{0,1:T(1,128)} %copy-done.12) | copy-start | bytes 3076
  252.1 3.7 %copy-start.9 = (f32[4,128,384]{2,1,0:T(8,128)S(1)}, f32[4,128,384]{2,1,0:T(8,128)}, u32[]{:S(2)}) copy-start(f32[4,128,384]{2,1,0:T(8,128)} %reduce-scatter.2.cloned.1.call-done) | copy-start | bytes 2359300
  296.7 7.2 %copy-start.1 = (bf16[64,2,12,1024]{3,1,2,0:T(2,128)(2,1)S(1)}, bf16[64,2,12,1024]{3,1,2,0:T(2,128)(2,1)}, u32[]{:S(2)}) copy-start(bf16[64,2,12,1024]{3,1,2,0:T(2,128)(2,1)} %param.13) | copy-start | bytes 9437188
Sparse Core Ops, SparseCore 0:
  14.6 78.2 all-gather.3
  171.0 74.7 reduce-scatter.1
  253.3 43.3 all-gather.5

commit v2 on v1

--- a/solution.py
+++ b/solution.py
@@ -163,34 +163,36 @@
     outgoing = jnp.dot(
         pick, my_width.reshape(number, -1), preferred_element_type=jnp.float32
     ).astype(weights.dtype)
-    outgoing = outgoing.reshape(n_own, pairs, 2 * piece_rows * width_part)
-    item_rows = peer_rows.reshape(n_own, pairs)
-    halves = 2
-    half = pairs // halves
-    pred_parts = []
+    chunks = TOUCH
+    per = TOUCH // chunks
+    part_pairs = n_dp * per
+    flat = 2 * piece_rows * width_part
+    item_rows = peer_rows.reshape(n_own, n_dp, chunks, per)
+    sig_all = sig_slots.reshape(n_dp, chunks, per, CAP, SITES)
+    cot_all = cot_slots.reshape(n_dp, chunks, per, CAP, SITES)
+    fetched = lax.all_to_all(
+        outgoing.reshape(n_own, pairs, flat), "own", split_axis=0, concat_axis=0, tiled=True
+    )
+    fetched = fetched.reshape(n_own, n_dp, chunks, per, flat)
+    sent = None
+    pieces = None
     table = None
-    fetched = [
-        lax.all_to_all(
-            outgoing[:, h * half : (h + 1) * half], "own", split_axis=0, concat_axis=0, tiled=True
-        )
-        for h in range(halves)
-    ]
-    sent = None
-    for h in range(halves):
-        chosen = slice(h * half, (h + 1) * half)
-        arrived = fetched[h]
-        arrived = arrived.reshape(n_own, half, 2, piece_rows, width_part)
-        arrived = arrived.transpose(1, 2, 0, 3, 4).reshape(half, 2, SITES, width_part)
+    pred_chunks = []
+    for c in range(chunks):
+        taken = fetched[:, :, c]
+        if pieces is not None:
+            taken, pieces = lax.optimization_barrier((taken, pieces))
+            sent = lax.all_to_all(pieces, "own", split_axis=0, concat_axis=0, tiled=True)
+        arrived = taken.reshape(n_own, part_pairs, 2, piece_rows, width_part)
+        arrived = arrived.transpose(1, 2, 0, 3, 4).reshape(part_pairs, 2, SITES, width_part)
         read_in = arrived[:, 0]
         read_out = arrived[:, 1]
-        sig_part = sig_slots[chosen]
-        cot_part = cot_slots[chosen]
+        sig_part = sig_all[:, c].reshape(part_pairs, CAP, SITES)
+        cot_part = cot_all[:, c].reshape(part_pairs, CAP, SITES)
         preact = jnp.einsum("kcs,ksw->kcw", sig_part, read_in, preferred_element_type=jnp.float32)
         gelu_val, slopes = gelu_parts(preact)
         hidden = gelu_val.astype(jnp.bfloat16)
-        pred_parts.append(
-            jnp.einsum("kcw,ksw->kcs", hidden, read_out, preferred_element_type=jnp.float32)
-        )
+        pred_part = jnp.einsum("kcw,ksw->kcs", hidden, read_out, preferred_element_type=jnp.float32)
         back_hidden = jnp.einsum(
             "kcs,ksw->kcw", cot_part, read_out, preferred_element_type=jnp.float32
         )
@@ -198,25 +200,18 @@
         grad_in = jnp.einsum("kcs,kcw->ksw", sig_part, back_pre, preferred_element_type=jnp.float32)
         grad_out = jnp.einsum("kcs,kcw->ksw", cot_part, hidden, preferred_element_type=jnp.float32)
         grads = jnp.stack([grad_in, grad_out], axis=1).astype(jnp.bfloat16)
-        if h + 1 < halves:
-            grads, fetched[h + 1] = lax.optimization_barrier((grads, fetched[h + 1]))
+        pred_part, grads = lax.optimization_barrier((pred_part, grads))
+        pred_chunks.append(lax.psum_scatter(pred_part, "dp", scatter_dimension=0, tiled=True))
         if sent is not None:
             grads, sent = lax.optimization_barrier((grads, sent))
-            table = sum_by_insertion(item_rows[:, :half].reshape(-1), sent, number)
-        if h == halves - 1:
-            pred_part = jnp.concatenate(pred_parts, axis=0)
-            pred_part, grads = lax.optimization_barrier((pred_part, grads))
-            pred_slots = lax.psum_scatter(pred_part, "dp", scatter_dimension=0, tiled=True)
-        pieces = grads.reshape(half, 2, n_own, piece_rows, width_part).transpose(2, 0, 1, 3, 4)
-        pieces = pieces.reshape(n_own, half, 2 * piece_rows * width_part)
-        arrived_grad = lax.all_to_all(pieces, "own", split_axis=0, concat_axis=0, tiled=True)
-        if h == halves - 1:
-            arrived_grad, pred_slots = lax.optimization_barrier((arrived_grad, pred_slots))
-            part = sum_by_insertion(item_rows[:, chosen].reshape(-1), arrived_grad, number)
-            table = part + table
-        else:
-            sent = arrived_grad
-    pred_slots = pred_slots.astype(jnp.bfloat16)
+            part = sum_by_insertion(item_rows[:, :, c - 1].reshape(-1), sent, number)
+            table = part if table is None else table + part
+        pieces = grads.reshape(part_pairs, 2, n_own, piece_rows, width_part)
+        pieces = pieces.transpose(2, 0, 1, 3, 4).reshape(n_own, part_pairs, flat)
+    sent = lax.all_to_all(pieces, "own", split_axis=0, concat_axis=0, tiled=True)
+    part = sum_by_insertion(item_rows[:, :, chunks - 1].reshape(-1), sent, number)
+    table = part if table is None else table + part
+    pred_slots = jnp.stack(pred_chunks, axis=1).reshape(TOUCH, CAP, SITES).astype(jnp.bfloat16)
     table = table.reshape(number, 2, piece_rows, width_part)
     own_params = my_width.astype(jnp.float32)
     fresh_part, new_moment1, new_moment2 = adam_step(own_params, moment1, moment2, table)

time: 316 us -> 354 us (1.12)
  blocking collectives: 47.9 us -> 109 us
  waiting for transfers between devices: 111 us -> 84.5 us
  matrix products: 29.3 us -> 40.8 us
  local copies, waits for them, and re-layouts: 74.3 us -> 63.6 us
    all_to_all x1 -> x2, blocking collectives: 47.9 us -> 109 us  [the longest x1 81.8 us: shards(): lax.all_to_all(outgoing.reshape(n_own, pairs, flat), 'own', split_axis=0,...]
    reshape x4 -> x0, local copies, waits for them, and re-layouts: 24.4 us -> none  [the longest x2 13.8 us: shards(): pieces = pieces.reshape(n_own, half, 2 * piece_rows * width_part)]
    reduce_scatter x1 -> x4, waiting for transfers between devices: 16.2 us -> 0.07 us  [shards(): lax.psum_scatter(pred_part, 'dp', scatter_dimension=0, tiled=True)]
    transpose x4 -> x8, local copies, waits for them, and re-layouts: 14.7 us -> 6.93 us  [the longest x4 5.34 us: shards(): pieces = pieces.transpose(2, 0, 1, 3, 4).reshape(n_own, part_pairs, flat)]
    all_gather x1, waiting for transfers between devices: 7.57 us -> 0.01 us  [shards(): lax.all_gather(stacked.reshape(TOUCH, CAP, 2 * SITES), 'dp', axis=0, tile...]
    all_to_all x2 -> x3, waiting for transfers between devices: 46 us -> 39.4 us  [shards(): lax.all_to_all(pieces, 'own', split_axis=0, concat_axis=0, tiled=True)]
    dot_general x2 -> x4, matrix products: 1.84 us -> 7.88 us  [shards(): jnp.einsum('kcw,ksw->kcs', hidden, read_out, preferred_element_type=jnp.f...]
    all_gather x1, waiting for transfers between devices: 39 us -> 45 us  [shards(): new_weights = lax.all_gather(fresh_part, 'dp', axis=0, tiled=False)]
  transfers between devices with their start and end apart: 6 -> 9, of which waited for: 6 -> 4; matrix products, arithmetic and copies ran while one was open for 27% -> 26% of each run, Pallas kernels for 0% -> 0%
where the time goes in v2:
time: 354 us; the launch traced here: 348 us
  blocking collectives  109 us (31%)
  waiting for transfers between devices  84.5 us (24%)
  local copies, waits for them, and re-layouts  63.6 us (18%)
  matrix products  40.8 us (12%)
  other arithmetic  21.1 us (6%)
  between operations  14.8 us (4%)
  starting transfers between devices  14.3 us (4%)
    all_to_all x1, blocking collectives, shards(): lax.all_to_all(outgoing.reshape(n_own, pairs, flat), 'own', split_axis=0,...  81.8 us
    all_gather x1, waiting for transfers between devices, shards(): new_weights = lax.all_gather(fresh_part, 'dp', axis=0, tiled=False)  45 us
    all_to_all x3, waiting for transfers between devices, shards(): lax.all_to_all(pieces, 'own', split_axis=0, concat_axis=0, tiled=True)  39.4 us
    all_to_all x1, blocking collectives, shards(): lax.all_to_all(pieces, 'own', split_axis=0, concat_axis=0, tiled=True)  27.5 us
    dot_general x4, matrix products, shards(): jnp.einsum('kcs,kcw->ksw', sig_part, back_pre, preferred_element_type=jnp...  13.6 us
    all_to_all x3, starting transfers between devices, shards(): lax.all_to_all(pieces, 'own', split_axis=0, concat_axis=0, tiled=True)  13.3 us
    unnamed x57, local copies, waits for them, and re-layouts  9.67 us
    another operation x4, other arithmetic, shards(): grads = jnp.stack([grad_in, grad_out], axis=1).astype(jnp.bfloat16)  9.07 us
  transfers between devices with their start and end apart: 9, of which 4 were waited for; matrix products, arithmetic and copies ran while one was open for 26% of the time, Pallas kernels for 0%

profile of v2, /device:TPU:1, one launch (start us, length us, event | category | flops | bytes accessed | tf_op | source)
XLA Modules:
  0.0 348.5 jit_solution(8736739569462419253)
XLA Ops:
  11.4 3.1 scatter_custom_fusion
  16.6 1.8 convolution_convert_fusion
  18.5 81.8 %all_to_all.25 = bf16[32,32,3072]{2,1,0:T(8,128)(2,1)S(1)} all-to-all(bf16[32,32,3072]{2,1,0:T(8,128)(2,1)S(1)} %bitcast.209), channel_id=1, replica_groups=mesh['dp'=8,'own'=32] {'own'}, dimensions={0} | all-to-all | bytes 12582912 | tf_op jit(solution)/shard_map/all_to_all | solution.py:173
  100.3 3.4 copy.181
  107.6 3.6 %fusion.137 = (bf16[32,128,384]{2,1,0:T(8,128)(2,1)S(1)}, bf16[32,128,384]{2,1,0:T(8,128)(2,1)S(1)}) fusion(bf16[32,128,768]{2,1,0:T(8,128)(2,1)} %all-gather.4.cloned.1.call-done), kind=kLoop, calls=%fused_computation.207 | loop fusion | bytes 12582912 | tf_op jit(solution)/shard_map/slice | solution.py:160
  115.5 3.5 %fusion.5 = bf16[8,1,384,128]{3,2,0,1:T(8,128)(2,1)} fusion(bf16[8,1,384,128]{3,0,2,1:T(8,128)(2,1)} %get-tuple-element.78, bf16[8,4,1,128,384]{4,3,1,0,2:T(8,128)(2,1)} %bitcast.240, bf16[8,4,1,128,384]{4,3,1,0,2:T(8,128)(2,1)} %bitcast.232, f32[8,128,128]{2,1,0:T(8,128)} %copy-done.18), kind=kOutput, calls=%fused_computation.28 | convolution fusion | flops 204210176 | bytes 3670016 | tf_op jit(solution)/shard_map/kcs,kcw->ksw/dot_general | solution.py:200
  119.0 2.9 fusion.23
  121.9 2.7 pad_maximum_fusion
  134.1 3.3 fusion.7
  137.5 2.5 pad_maximum_fusion.1
  141.7 3.9 %all-to-all-start.1 = ((bf16[32,8,3072]{2,1,0:T(8,128)(2,1)}), bf16[32,8,3072]{2,1,0:T(8,128)(2,1)S(1)}, u32[]{:S(2)}, u32[]{:S(2)}) async-start(bf16[32,8,3072]{2,1,0:T(8,128)(2,1)} %bitcast.213), calls=%async_computation.3 | async-start | bytes 3145728 | tf_op jit(solution)/shard_map/all_to_all | solution.py:185
  145.6 4.8 %copy_bitcast_fusion.1 = (bf16[32,8,1,3072]{3,1,0,2:T(8,128)(2,1)}, bf16[32,8,1,3072]{3,1,0,2:T(8,128)(2,1)}) fusion(bf16[32,8,1,1,3072]{4,0,2,1,3:T(8,128)(2,1)S(1)} %get-tuple-element.68, bf16[32,8,1,1,3072]{4,0,2,1,3:T(8,128)(2,1)} %get-tuple-element.69), kind=kLoop, calls=%fused_computation.16 | loop fusion | bytes 6291456 | tf_op jit(solution)/shard_map/squeeze | solution.py:182
  150.4 17.8 %all-to-all-done.1 = bf16[32,8,3072]{2,1,0:T(8,128)(2,1)S(1)} async-done(((bf16[32,8,3072]{2,1,0:T(8,128)(2,1)}), bf16[32,8,3072]{2,1,0:T(8,128)(2,1)S(1)}, u32[]{:S(2)}, u32[]{:S(2)}) %all-to-all-start.1) | async-done | bytes 1572896 | tf_op jit(solution)/shard_map/all_to_all | solution.py:185
  168.2 2.4 copy.201
  177.8 3.3 fusion.9
  181.1 2.5 pad_maximum_fusion.2
  185.3 27.5 %all_to_all.26 = bf16[32,8,3072]{2,1,0:T(8,128)(2,1)S(1)} all-to-all(bf16[32,8,3072]{2,1,0:T(8,128)(2,1)} %bitcast.215), channel_id=1, replica_groups=mesh['dp'=8,'own'=32] {'own'}, dimensions={0} | all-to-all | bytes 3145728 | tf_op jit(solution)/shard_map/all_to_all | solution.py:185
  217.1 4.5 %all-to-all-start.3 = ((bf16[32,8,3072]{2,1,0:T(8,128)(2,1)}), bf16[32,8,3072]{2,1,0:T(8,128)(2,1)}, u32[]{:S(2)}, u32[]{:S(2)}) async-start(bf16[32,8,3072]{2,1,0:T(8,128)(2,1)} %bitcast.214), calls=%async_computation.7 | async-start | bytes 3145728 | tf_op jit(solution)/shard_map/all_to_all | solution.py:185
  221.6 2.4 fusion.139
  224.0 2.3 fusion.19
  226.3 3.5 %fusion.11 = bf16[8,1,384,128]{3,2,0,1:T(8,128)(2,1)} fusion(bf16[8,1,384,128]{3,0,2,1:T(8,128)(2,1)} %get-tuple-element.72, bf16[8,4,1,128,384]{4,3,1,0,2:T(8,128)(2,1)} %bitcast.246, bf16[8,4,1,128,384]{4,3,1,0,2:T(8,128)(2,1)} %bitcast.237, f32[8,128,128]{2,1,0:T(8,128)} %fusion.19), kind=kOutput, calls=%fused_computation.34 | convolution fusion | flops 204210176 | bytes 3670016 | tf_op jit(solution)/shard_map/kcs,kcw->ksw/dot_general | solution.py:200
  229.8 1.9 fusion.12
  235.2 8.8 %all-to-all-done.3 = bf16[32,8,3072]{2,1,0:T(8,128)(2,1)} async-done(((bf16[32,8,3072]{2,1,0:T(8,128)(2,1)}), bf16[32,8,3072]{2,1,0:T(8,128)(2,1)}, u32[]{:S(2)}, u32[]{:S(2)}) %all-to-all-start.3) | async-done | bytes 1572896 | tf_op jit(solution)/shard_map/all_to_all | solution.py:185
  244.0 2.4 copy.224
  247.8 5.0 %all-to-all-start.4 = ((bf16[32,8,3072]{2,1,0:T(8,128)(2,1)}), bf16[32,8,3072]{2,1,0:T(8,128)(2,1)}, u32[]{:S(2)}, u32[]{:S(2)}) async-start(bf16[32,8,3072]{2,1,0:T(8,128)(2,1)} %bitcast.212), calls=%async_computation.8 | async-start | bytes 3145728 | tf_op jit(solution)/shard_map/all_to_all | solution.py:211
  261.0 1.8 convolution_add_fusion.1
  262.8 12.7 %all-to-all-done.4 = bf16[32,8,3072]{2,1,0:T(8,128)(2,1)} async-done(((bf16[32,8,3072]{2,1,0:T(8,128)(2,1)}), bf16[32,8,3072]{2,1,0:T(8,128)(2,1)}, u32[]{:S(2)}, u32[]{:S(2)}) %all-to-all-start.4) | async-done | bytes 1572896 | tf_op jit(solution)/shard_map/all_to_all | solution.py:211
  275.6 1.8 convolution_add_fusion
  277.6 2.2 subtract_convert_fusion
  287.4 1.8 gather_fusion
  289.3 45.0 %all-gather.6.cloned.1.call-done = bf16[512,2,12,128]{3,1,2,0:T(2,128)(2,1)} async-done(((bf16[64,2,12,128]{3,1,2,0:T(2,128)(2,1)}), bf16[512,2,12,128]{3,1,2,0:T(2,128)(2,1)}) %all-gather.6.cloned.1.call-update) | async-done | bytes 3145744 | tf_op jit(solution)/shard_map/all_gather | solution.py:218
  334.2 7.2 %copy.296 = bf16[8,64,12,1,2,128]{5,4,0,3,2,1:T(2,128)(2,1)} copy(bf16[8,64,12,1,2,128]{5,4,3,2,1,0:T(2,128)(2,1)} %bitcast.228) | data formatting | bytes 6291456 | tf_op jit(solution)/shard_map/reshape | solution.py:219
  (137 shorter events, 59.5 us)
Async XLA Ops:
  7.2 8.5 %copy-start = (bf16[64,2,12,1024]{3,1,2,0:T(2,128)(2,1)S(1)}, bf16[64,2,12,1024]{3,1,2,0:T(2,128)(2,1)}, u32[]{:S(2)}) copy-start(bf16[64,2,12,1024]{3,1,2,0:T(2,128)(2,1)} %param.13) | copy-start | bytes 9437188
  7.2 7.4 %copy-start.20 = (s32[256,4]{0,1:T(4,128)S(1)}, s32[256,4]{0,1:T(4,128)}, u32[]{:S(2)}) copy-start(s32[256,4]{0,1:T(4,128)} %param.11) | copy-start | bytes 12292
  7.2 7.4 %copy-start.26 = (s32[64]{0:T(128)S(1)}, s32[64]{0:T(128)}, u32[]{:S(2)}) copy-start(s32[64]{0:T(128)} %param.12) | copy-start | bytes 772
  7.2 100.4 %all-gather.4.cloned.1.call-start = ((), (), s32[]{:S(2)}) async-start(), calls=%async_computation.9 | async-start | bytes 7077888 | tf_op jit(solution)/shard_map/all_gather | solution.py:157
  11.4 3.1 copy-start.24
  14.5 266.4 %reduce-scatter.5.cloned.1.call-start = ((), (), s32[]{:S(2)}) async-start(), calls=%async_computation.10 | async-start | bytes 1769472 | tf_op jit(solution)/shard_map/reduce_scatter | solution.py:204
  107.6 5.3 %copy-start.11 = (bf16[8,1,384,128]{3,0,2,1:T(8,128)(2,1)S(1)}, bf16[8,1,384,128]{3,0,2,1:T(8,128)(2,1)}, u32[]{:S(2)}) copy-start(bf16[8,1,384,128]{3,0,2,1:T(8,128)(2,1)} %get-tuple-element.77) | copy-start | bytes 2359300
  111.2 1.7 copy-start.7
  111.2 4.2 %copy-start.6 = (bf16[32,128,384]{2,1,0:T(8,128)(2,1)}, bf16[32,128,384]{2,1,0:T(8,128)(2,1)S(1)}, u32[]{:S(2)}) copy-start(bf16[32,128,384]{2,1,0:T(8,128)(2,1)S(1)} %get-tuple-element.65) | copy-start | bytes 9437188
  113.3 0.8 copy-start.18
  124.7 157.3 %reduce-scatter.7.cloned.1.call-start = ((), (), s32[]{:S(2)}) async-start(), calls=%async_computation.11 | async-start | bytes 1769472 | tf_op jit(solution)/shard_map/reduce_scatter | solution.py:204
  125.2 1.4 copy-start.3
  132.4 1.7 copy-start.9
  137.5 2.5 copy-start.15
  141.7 26.5 %all-to-all-start.1 = ((bf16[32,8,3072]{2,1,0:T(8,128)(2,1)}), bf16[32,8,3072]{2,1,0:T(8,128)(2,1)S(1)}, u32[]{:S(2)}, u32[]{:S(2)}) async-start(bf16[32,8,3072]{2,1,0:T(8,128)(2,1)} %bitcast.213), calls=%async_computation.3 | async-start | bytes 3145728 | tf_op jit(solution)/shard_map/all_to_all | solution.py:185
  145.6 137.3 %reduce-scatter.9.cloned.1.call-start = ((), (), s32[]{:S(2)}) async-start(), calls=%async_computation.12 | async-start | bytes 1769472 | tf_op jit(solution)/shard_map/reduce_scatter | solution.py:204
  170.7 2.0 copy-start.5
  176.0 1.8 copy-start.10
  181.1 2.5 copy-start.17
  185.3 27.5 %copy-start.2 = (bf16[8,2,384,128]{3,2,0,1:T(8,128)(2,1)S(1)}, bf16[8,2,384,128]{3,2,0,1:T(8,128)(2,1)}, u32[]{:S(2)}) copy-start(bf16[8,2,384,128]{3,2,0,1:T(8,128)(2,1)} %pad_maximum_fusion.2) | copy-start | bytes 4718596
  213.8 2.0 copy-start.4
  217.1 26.9 %all-to-all-start.3 = ((bf16[32,8,3072]{2,1,0:T(8,128)(2,1)}), bf16[32,8,3072]{2,1,0:T(8,128)(2,1)}, u32[]{:S(2)}, u32[]{:S(2)}) async-start(bf16[32,8,3072]{2,1,0:T(8,128)(2,1)} %bitcast.214), calls=%async_computation.7 | async-start | bytes 3145728 | tf_op jit(solution)/shard_map/all_to_all | solution.py:185
  221.6 64.8 %reduce-scatter.11.cloned.1.call-start = ((), (), s32[]{:S(2)}) async-start(), calls=%async_computation.13 | async-start | bytes 1769472 | tf_op jit(solution)/shard_map/reduce_scatter | solution.py:204
  229.8 1.9 copy-start.12
  231.7 1.3 copy-start.8
  231.7 1.8 copy-start.13
  247.8 27.8 %all-to-all-start.4 = ((bf16[32,8,3072]{2,1,0:T(8,128)(2,1)}), bf16[32,8,3072]{2,1,0:T(8,128)(2,1)}, u32[]{:S(2)}, u32[]{:S(2)}) async-start(bf16[32,8,3072]{2,1,0:T(8,128)(2,1)} %bitcast.212), calls=%async_computation.8 | async-start | bytes 3145728 | tf_op jit(solution)/shard_map/all_to_all | solution.py:211
  252.7 81.5 %all-gather.6.cloned.1.call-start = ((), (), s32[]{:S(2)}) async-start(), calls=%async_computation.14 | async-start | bytes 3538944 | tf_op jit(solution)/shard_map/all_gather | solution.py:218
  259.3 1.1 copy-start.23
  261.0 14.5 %copy-start.21 = (s32[256]{0:T(256)S(1)}, s32[256]{0:T(256)}, u32[]{:S(2)}) copy-start(s32[256]{0:T(256)} %eq.141) | copy-start | bytes 3076
  277.6 3.3 copy-start.25
  334.2 7.2 %copy-start.1 = (bf16[64,2,12,1024]{3,1,2,0:T(2,128)(2,1)S(1)}, bf16[64,2,12,1024]{3,1,2,0:T(2,128)(2,1)}, u32[]{:S(2)}) copy-start(bf16[64,2,12,1024]{3,1,2,0:T(2,128)(2,1)} %param.13) | copy-start | bytes 9437188
  (4 other events, 3.0 us)
Sparse Core Ops, SparseCore 0:
  14.6 78.2 all-gather.3
  124.8 35.6 reduce-scatter.4
  163.1 38.9 reduce-scatter.6
  204.5 39.1 reduce-scatter.8
  246.6 38.9 reduce-scatter.10
  287.3 46.8 all-gather.5

commit v3 on v1

--- a/solution.py
+++ b/solution.py
@@ -15,37 +15,27 @@
 
 MESH = pl.DeviceIdType.MESH
 
-def _a2a_kernel(n_dp, n_own, full, x_ref, o_ref, send_sems, recv_sems, local_sem):
-    dp_at = lax.axis_index("dp")
+def _gather_kernel(n, x_ref, o_ref, send_sems, recv_sems, local_sem):
+    me = lax.axis_index("dp")
     own_at = lax.axis_index("own")
-    if full:
-        n = n_dp * n_own
-        me = dp_at * n_own + own_at
-        def dev(k):
-            return (k // n_own, k % n_own)
-    else:
-        n = n_own
-        me = own_at
-        def dev(k):
-            return (dp_at, k)
     barrier = pltpu.get_barrier_semaphore()
 
     def greet(i, c):
         peer = lax.rem(me + i, n)
-        pl.semaphore_signal(barrier, 1, device_id=dev(peer), device_id_type=MESH)
+        pl.semaphore_signal(barrier, 1, device_id=(peer, own_at), device_id_type=MESH)
         return c
 
     lax.fori_loop(1, n, greet, 0)
     pl.semaphore_wait(barrier, n - 1)
-    local = pltpu.make_async_copy(x_ref.at[me], o_ref.at[me], local_sem)
+    local = pltpu.make_async_copy(x_ref, o_ref.at[me], local_sem)
     local.start()
 
     def send(i, c):
         peer = lax.rem(me + i, n)
         pltpu.make_async_remote_copy(
-            src_ref=x_ref.at[peer], dst_ref=o_ref.at[me],
+            src_ref=x_ref, dst_ref=o_ref.at[me],
             send_sem=send_sems.at[peer], recv_sem=recv_sems.at[me],
-            device_id=dev(peer), device_id_type=MESH,
+            device_id=(peer, own_at), device_id_type=MESH,
         ).start()
         return c
 
@@ -55,14 +45,14 @@
         peer = lax.rem(me + i, n)
         src = lax.rem(me + n - i, n)
         pltpu.make_async_remote_copy(
-            src_ref=x_ref.at[peer], dst_ref=o_ref.at[src],
+            src_ref=x_ref, dst_ref=o_ref.at[src],
             send_sem=send_sems.at[peer], recv_sem=recv_sems.at[src],
-            device_id=dev(peer), device_id_type=MESH,
+            device_id=(peer, own_at), device_id_type=MESH,
         ).wait_send()
         pltpu.make_async_remote_copy(
-            src_ref=x_ref.at[peer], dst_ref=o_ref.at[src],
+            src_ref=x_ref, dst_ref=o_ref.at[src],
             send_sem=send_sems.at[peer], recv_sem=recv_sems.at[src],
-            device_id=dev(src), device_id_type=MESH,
+            device_id=(src, own_at), device_id_type=MESH,
         ).wait_recv()
         return c
 
@@ -70,11 +60,10 @@
     local.wait()
 
 
-def exchange(x, n_dp, n_own, full, cid):
-    n = x.shape[0]
+def gather_dp(x, n, cid):
     return pl.pallas_call(
-        functools.partial(_a2a_kernel, n_dp, n_own, full),
-        out_shape=jax.ShapeDtypeStruct(x.shape, x.dtype),
+        functools.partial(_gather_kernel, n),
+        out_shape=jax.ShapeDtypeStruct((n,) + x.shape, x.dtype),
         in_specs=[pl.BlockSpec(memory_space=pl.ANY)],
         out_specs=pl.BlockSpec(memory_space=pl.ANY),
         scratch_shapes=[
@@ -220,7 +209,7 @@
     table = table.reshape(number, 2, piece_rows, width_part)
     own_params = my_width.astype(jnp.float32)
     fresh_part, new_moment1, new_moment2 = adam_step(own_params, moment1, moment2, table)
-    new_weights = lax.all_gather(fresh_part, "dp", axis=0, tiled=False)
+    new_weights = gather_dp(fresh_part, n_dp, 0)
     new_weights = new_weights.transpose(1, 2, 3, 0, 4).reshape(weights.shape)
     predicted = pred_slots.reshape(TOUCH * CAP, SITES)[places]
     return (predicted, new_weights, new_moment1, new_moment2)

time: 316 us -> 377 us (1.19)
  Pallas kernels: 0 us -> 95.4 us
  waiting for transfers between devices: 111 us -> 71.2 us
    pallas_call x0 -> x1, Pallas kernels: none -> 95.4 us  [gather_dp(): pl.pallas_call(functools.partial(_gather_kernel, n), out_shape=jax.ShapeD...]
    all_gather x1 -> x0, waiting for transfers between devices: 39 us -> none  [shards(): new_weights = lax.all_gather(fresh_part, 'dp', axis=0, tiled=False)]
    unnamed x33 -> x35, local copies, waits for them, and re-layouts: 5.39 us -> 16.8 us
    reshape x1 -> x0, local copies, waits for them, and re-layouts: 7.16 us -> none  [shards(): new_weights = new_weights.transpose(1, 2, 3, 0, 4).reshape(weights.shape)]
  transfers between devices with their start and end apart: 6 -> 5, of which waited for: 6 -> 5; matrix products, arithmetic and copies ran while one was open for 27% -> 22% of each run, Pallas kernels for 0% -> 0%
where the time goes in v3:
time: 377 us; the launch traced here: 371 us
  Pallas kernels  95.4 us (25%)
  local copies, waits for them, and re-layouts  77.5 us (21%)
  waiting for transfers between devices  71.2 us (19%)
  blocking collectives  47.9 us (13%)
  matrix products  29.4 us (8%)
  other arithmetic  20.5 us (5%)
  starting transfers between devices  14.9 us (4%)
  between operations  14.5 us (4%)
    pallas_call x1, Pallas kernels, gather_dp(): pl.pallas_call(functools.partial(_gather_kernel, n), out_shape=jax.ShapeD...  95.4 us
    all_to_all x1, blocking collectives, shards(): lax.all_to_all(outgoing[:, h * half:(h + 1) * half], 'own', split_axis=0,...  47.9 us
    all_to_all x2, waiting for transfers between devices, shards(): lax.all_to_all(pieces, 'own', split_axis=0, concat_axis=0, tiled=True)  45.3 us
    unnamed x35, local copies, waits for them, and re-layouts  16.8 us
    reduce_scatter x1, waiting for transfers between devices, shards(): lax.psum_scatter(pred_part, 'dp', scatter_dimension=0, tiled=True)  16.2 us
    reshape x2, local copies, waits for them, and re-layouts, shards(): pieces = pieces.reshape(n_own, half, 2 * piece_rows * width_part)  13.8 us
    dot_general x2, matrix products, shards(): jnp.einsum('kcs,kcw->ksw', sig_part, back_pre, preferred_element_type=jnp...  11.1 us
    reshape x2, local copies, waits for them, and re-layouts, shards(): arrived = arrived.reshape(n_own, half, 2, piece_rows, width_part)  10.6 us
  transfers between devices with their start and end apart: 5, of which 5 were waited for; matrix products, arithmetic and copies ran while one was open for 22% of the time, Pallas kernels for 0%

profile of v3, /device:TPU:1, one launch (start us, length us, event | category | flops | bytes accessed | tf_op | source)
XLA Modules:
  0.0 371.5 jit_solution(52263704850573199)
XLA Ops:
  11.4 3.1 scatter_custom_fusion
  19.7 47.9 %all_to_all.20 = bf16[32,16,3072]{2,1,0:T(8,128)(2,1)} all-to-all(bf16[32,16,3072]{2,1,0:T(8,128)(2,1)S(1)} %get-tuple-element.46), channel_id=1, replica_groups=mesh['dp'=8,'own'=32] {'own'}, dimensions={0} | all-to-all | bytes 6291456 | tf_op jit(solution)/shard_map/all_to_all | solution.py:162
  67.6 4.5 %all-to-all-start.1 = ((bf16[32,16,3072]{2,1,0:T(8,128)(2,1)}), bf16[32,16,3072]{2,1,0:T(8,128)(2,1)S(1)}, u32[]{:S(2)}, u32[]{:S(2)}) async-start(bf16[32,16,3072]{2,1,0:T(8,128)(2,1)} %get-tuple-element.45), calls=%async_computation.1 | async-start | bytes 6291456 | tf_op jit(solution)/shard_map/all_to_all | solution.py:162
  72.1 6.8 %reshape.115 = bf16[32,16,2,12,128]{4,3,2,1,0:T(8,128)(2,1)} reshape(bf16[32,16,3072]{2,1,0:T(8,128)(2,1)} %all_to_all.20) | data formatting | bytes 6291456 | tf_op jit(solution)/shard_map/reshape | solution.py:171
  78.9 4.2 %copy.113 = bf16[16,2,32,12,128]{4,0,3,2,1:T(8,128)(2,1)S(1)} copy(bf16[16,2,32,12,128]{4,3,1,0,2:T(8,128)(2,1)} %bitcast.76) | data formatting | bytes 6291456 | tf_op jit(solution)/shard_map/transpose | solution.py:172
  85.4 7.6 %all-gather.2.cloned.1.call-done = bf16[32,128,768]{2,1,0:T(8,128)(2,1)} async-done(((bf16[4,128,768]{2,1,0:T(8,128)(2,1)}), bf16[32,128,768]{2,1,0:T(8,128)(2,1)}) %all-gather.2.cloned.1.call-update) | async-done | bytes 6291472 | tf_op jit(solution)/shard_map/all_gather | solution.py:146
  92.9 2.7 fusion.1
  96.6 3.4 fusion.3
  100.0 5.7 %fusion.2 = bf16[16,1,384,128]{3,2,0,1:T(8,128)(2,1)} fusion(bf16[32,128,768]{2,1,0:T(8,128)(2,1)} %all-gather.2.cloned.1.call-done, bf16[16,1,384,128]{3,0,2,1:T(8,128)(2,1)} %get-tuple-element.49, f32[16,128,128]{2,1,0:T(8,128)} %copy-done.5), kind=kOutput, calls=%fused_computation.22 | convolution fusion | flops 408420352 | bytes 7340032 | tf_op jit(solution)/shard_map/kcs,kcw->ksw/dot_general | solution.py:187
  105.8 3.9 %pad_maximum_fusion.1 = bf16[16,2,384,128]{3,2,0,1:T(8,128)(2,1)} fusion(bf16[16,1,384,128]{3,2,0,1:T(8,128)(2,1)} %fusion.3, bf16[16,1,384,128]{3,2,0,1:T(8,128)(2,1)} %fusion.2), kind=kLoop, calls=%fused_computation.5 | loop fusion | flops 1572864 | bytes 6291456 | tf_op jit(solution)/shard_map/stack | solution.py:189
  111.8 3.9 %copy.123 = bf16[16,2,384,128]{3,0,2,1:T(8,128)(2,1)S(1)} copy(bf16[16,2,384,128]{3,2,0,1:T(8,128)(2,1)} %pad_maximum_fusion.1) | data formatting | bytes 6291456 | tf_op jit(solution)/shard_map/optimization_barrier | solution.py:191
  115.7 3.1 copy.124
  118.8 6.8 %reshape.120 = bf16[32,16,3072]{2,1,0:T(8,128)(2,1)} reshape(bf16[32,16,2,12,128]{4,3,2,1,0:T(8,128)(2,1)} %copy.124) | data formatting | bytes 6291456 | tf_op jit(solution)/shard_map/reshape | solution.py:200
  125.5 5.5 %all-to-all-start.2 = ((bf16[32,16,3072]{2,1,0:T(8,128)(2,1)}), bf16[32,16,3072]{2,1,0:T(8,128)(2,1)}, u32[]{:S(2)}, u32[]{:S(2)}) async-start(bf16[32,16,3072]{2,1,0:T(8,128)(2,1)} %reshape.120), calls=%async_computation.2 | async-start | bytes 6291456 | tf_op jit(solution)/shard_map/all_to_all | solution.py:201
  131.1 3.8 %reshape.117 = bf16[32,16,2,12,128]{4,3,2,1,0:T(8,128)(2,1)} reshape(bf16[32,16,3072]{2,1,0:T(8,128)(2,1)S(1)} %all-to-all-done.1) | data formatting | bytes 6291456 | tf_op jit(solution)/shard_map/reshape | solution.py:171
  134.9 4.2 %copy.118 = bf16[16,2,32,12,128]{4,0,3,2,1:T(8,128)(2,1)S(1)} copy(bf16[16,2,32,12,128]{4,3,1,0,2:T(8,128)(2,1)} %bitcast.77) | data formatting | bytes 6291456 | tf_op jit(solution)/shard_map/transpose | solution.py:172
  146.4 5.3 %fusion.4 = bf16[16,1,384,128]{3,2,0,1:T(8,128)(2,1)} fusion(bf16[32,128,768]{2,1,0:T(8,128)(2,1)} %all-gather.2.cloned.1.call-done, bf16[16,1,384,128]{3,0,2,1:T(8,128)(2,1)S(1)} %copy-done.3, f32[16,128,128]{2,1,0:T(8,128)} %copy-done.7), kind=kOutput, calls=%fused_computation.24 | convolution fusion | flops 408420352 | bytes 7340032 | tf_op jit(solution)/shard_map/kcs,kcw->ksw/dot_general | solution.py:187
  151.7 3.5 pad_maximum_fusion.2
  157.8 3.3 pad_maximum_fusion
  161.1 9.8 %all-to-all-done.2 = bf16[32,16,3072]{2,1,0:T(8,128)(2,1)} async-done(((bf16[32,16,3072]{2,1,0:T(8,128)(2,1)}), bf16[32,16,3072]{2,1,0:T(8,128)(2,1)}, u32[]{:S(2)}, u32[]{:S(2)}) %all-to-all-start.2) | async-done | bytes 3145760 | tf_op jit(solution)/shard_map/all_to_all | solution.py:201
  170.9 3.9 %copy.125 = bf16[16,2,384,128]{3,0,2,1:T(8,128)(2,1)S(1)} copy(bf16[16,2,384,128]{3,2,0,1:T(8,128)(2,1)} %pad_maximum_fusion.2) | data formatting | bytes 6291456 | tf_op jit(solution)/shard_map/optimization_barrier | solution.py:197
  174.8 3.1 copy.126
  177.9 7.1 %reshape.122 = bf16[32,16,3072]{2,1,0:T(8,128)(2,1)} reshape(bf16[32,16,2,12,128]{4,3,2,1,0:T(8,128)(2,1)} %copy.126) | data formatting | bytes 6291456 | tf_op jit(solution)/shard_map/reshape | solution.py:200
  185.0 4.8 %all-to-all-start.3 = ((bf16[32,16,3072]{2,1,0:T(8,128)(2,1)}), bf16[32,16,3072]{2,1,0:T(8,128)(2,1)S(1)}, u32[]{:S(2)}, u32[]{:S(2)}) async-start(bf16[32,16,3072]{2,1,0:T(8,128)(2,1)} %reshape.122), calls=%async_computation.3 | async-start | bytes 6291456 | tf_op jit(solution)/shard_map/all_to_all | solution.py:201
  194.0 35.6 %all-to-all-done.3 = bf16[32,16,3072]{2,1,0:T(8,128)(2,1)S(1)} async-done(((bf16[32,16,3072]{2,1,0:T(8,128)(2,1)}), bf16[32,16,3072]{2,1,0:T(8,128)(2,1)S(1)}, u32[]{:S(2)}, u32[]{:S(2)}) %all-to-all-start.3) | async-done | bytes 3145760 | tf_op jit(solution)/shard_map/all_to_all | solution.py:201
  229.6 16.2 %reduce-scatter.2.cloned.1.call-done = f32[4,128,384]{2,1,0:T(8,128)} async-done(((f32[32,128,384]{2,1,0:T(8,128)}), f32[4,128,384]{2,1,0:T(8,128)}) %reduce-scatter.2.cloned.1.call-update) | async-done | bytes 786448 | tf_op jit(solution)/shard_map/reduce_scatter | solution.py:198
  247.2 2.6 convolution_add_fusion
  250.0 3.1 subtract_convert_fusion
  253.2 95.4 %shard_map.111 = bf16[8,64,2,12,128]{4,3,2,1,0:T(8,128)(2,1)} custom-call(bf16[64,2,12,128]{3,2,1,0:T(8,128)(2,1)} %get-tuple-element.42.x_ref), custom_call_target="tpu_custom_call" | custom-call | tf_op jit(solution)/shard_map/pallas_call | solution.py:64
  348.6 5.8 %copy.140 = bf16[64,2,12,8,128]{4,3,1,2,0:T(8,128)(2,1)S(1)} copy(bf16[64,2,12,8,128]{4,2,1,0,3:T(8,128)(2,1)} %bitcast.78) | data formatting | bytes 6291456
  354.4 2.9 reshape.144
  357.3 2.7 copy.134
  (74 shorter events, 34.7 us)
Async XLA Ops:
  7.2 7.4 %copy-start = (bf16[64,2,12,1024]{3,1,2,0:T(2,128)(2,1)S(1)}, bf16[64,2,12,1024]{3,1,2,0:T(2,128)(2,1)}, u32[]{:S(2)}) copy-start(bf16[64,2,12,1024]{3,1,2,0:T(2,128)(2,1)} %param.13) | copy-start | bytes 9437188
  7.2 8.0 %copy-start.11 = (s32[256,4]{0,1:T(4,128)S(1)}, s32[256,4]{0,1:T(4,128)}, u32[]{:S(2)}) copy-start(s32[256,4]{0,1:T(4,128)} %param.11) | copy-start | bytes 12292
  7.2 8.0 %copy-start.14 = (s32[64]{0:T(128)S(1)}, s32[64]{0:T(128)}, u32[]{:S(2)}) copy-start(s32[64]{0:T(128)} %param.12) | copy-start | bytes 772
  7.2 85.7 %all-gather.2.cloned.1.call-start = ((), (), s32[]{:S(2)}) async-start(), calls=%async_computation.5 | async-start | bytes 7077888 | tf_op jit(solution)/shard_map/all_gather | solution.py:146
  11.4 3.1 copy-start.13
  67.6 44.2 %all-to-all-start.1 = ((bf16[32,16,3072]{2,1,0:T(8,128)(2,1)}), bf16[32,16,3072]{2,1,0:T(8,128)(2,1)S(1)}, u32[]{:S(2)}, u32[]{:S(2)}) async-start(bf16[32,16,3072]{2,1,0:T(8,128)(2,1)} %get-tuple-element.45), calls=%async_computation.1 | async-start | bytes 6291456 | tf_op jit(solution)/shard_map/all_to_all | solution.py:162
  95.6 1.0 copy-start.5
  125.5 45.3 %all-to-all-start.2 = ((bf16[32,16,3072]{2,1,0:T(8,128)(2,1)}), bf16[32,16,3072]{2,1,0:T(8,128)(2,1)}, u32[]{:S(2)}, u32[]{:S(2)}) async-start(bf16[32,16,3072]{2,1,0:T(8,128)(2,1)} %reshape.120), calls=%async_computation.2 | async-start | bytes 6291456 | tf_op jit(solution)/shard_map/all_to_all | solution.py:201
  131.0 114.8 %reduce-scatter.2.cloned.1.call-start = ((), (), s32[]{:S(2)}) async-start(), calls=%async_computation.6 | async-start | bytes 7077888 | tf_op jit(solution)/shard_map/reduce_scatter | solution.py:198
  143.0 1.0 copy-start.7
  144.0 2.4 copy-start.3
  151.7 3.5 copy-start.4
  151.7 3.5 copy-start.8
  155.2 1.4 copy-start.2
  155.2 1.7 copy-start.6
  185.0 44.6 %all-to-all-start.3 = ((bf16[32,16,3072]{2,1,0:T(8,128)(2,1)}), bf16[32,16,3072]{2,1,0:T(8,128)(2,1)S(1)}, u32[]{:S(2)}, u32[]{:S(2)}) async-start(bf16[32,16,3072]{2,1,0:T(8,128)(2,1)} %reshape.122), calls=%async_computation.3 | async-start | bytes 6291456 | tf_op jit(solution)/shard_map/all_to_all | solution.py:201
  193.3 53.8 %copy-start.12 = (s32[512]{0:T(512)S(1)}, s32[512]{0:T(512)}, u32[]{:S(2)}) copy-start(s32[512]{0:T(512)} %eq.103) | copy-start | bytes 6148
  247.2 2.9 copy-start.10
  357.3 5.2 %copy-start.9 = (f32[4,128,384]{2,1,0:T(8,128)S(1)}, f32[4,128,384]{2,1,0:T(8,128)}, u32[]{:S(2)}) copy-start(f32[4,128,384]{2,1,0:T(8,128)} %reduce-scatter.2.cloned.1.call-done) | copy-start | bytes 2359300
  357.3 7.0 %copy-start.1 = (bf16[64,2,12,1024]{3,1,2,0:T(2,128)(2,1)S(1)}, bf16[64,2,12,1024]{3,1,2,0:T(2,128)(2,1)}, u32[]{:S(2)}) copy-start(bf16[64,2,12,1024]{3,1,2,0:T(2,128)(2,1)} %param.13) | copy-start | bytes 9437188
Sparse Core Ops, SparseCore 0:
  14.6 78.2 all-gather.1
  171.0 74.7 reduce-scatter.1

commit v4 on v1

--- a/solution.py
+++ b/solution.py
@@ -206,7 +206,9 @@
         if h == halves - 1:
             pred_part = jnp.concatenate(pred_parts, axis=0)
             pred_part, grads = lax.optimization_barrier((pred_part, grads))
-            pred_slots = lax.psum_scatter(pred_part, "dp", scatter_dimension=0, tiled=True)
+            pred_slots = lax.psum_scatter(
+                pred_part.astype(jnp.bfloat16), "dp", scatter_dimension=0, tiled=True
+            )
         pieces = grads.reshape(half, 2, n_own, piece_rows, width_part).transpose(2, 0, 1, 3, 4)
         pieces = pieces.reshape(n_own, half, 2 * piece_rows * width_part)
         arrived_grad = lax.all_to_all(pieces, "own", split_axis=0, concat_axis=0, tiled=True)

time: 316 us -> 303 us (0.959)
  waiting for transfers between devices: 111 us -> 100 us
    reduce_scatter x1, waiting for transfers between devices: 16.2 us -> 0.01 us  [shards(): lax.psum_scatter(pred_part.astype(jnp.bfloat16), 'dp', scatter_dimension=...]
    all_to_all x2, waiting for transfers between devices: 46 us -> 49.2 us  [shards(): lax.all_to_all(pieces, 'own', split_axis=0, concat_axis=0, tiled=True)]
  transfers between devices with their start and end apart: 6 -> 6, of which waited for: 6 -> 5; matrix products, arithmetic and copies ran while one was open for 27% -> 28% of each run, Pallas kernels for 0% -> 0%
where the time goes in v4:
time: 303 us; the launch traced here: 297 us
  waiting for transfers between devices  100 us (33%)
  local copies, waits for them, and re-layouts  72.5 us (24%)
  blocking collectives  47.9 us (16%)
  matrix products  30.5 us (10%)
  other arithmetic  17.7 us (6%)
  between operations  14.5 us (5%)
  starting transfers between devices  14.2 us (5%)
    all_to_all x2, waiting for transfers between devices, shards(): lax.all_to_all(pieces, 'own', split_axis=0, concat_axis=0, tiled=True)  49.2 us
    all_to_all x1, blocking collectives, shards(): lax.all_to_all(outgoing[:, h * half:(h + 1) * half], 'own', split_axis=0,...  47.9 us
    all_gather x1, waiting for transfers between devices, shards(): new_weights = lax.all_gather(fresh_part, 'dp', axis=0, tiled=False)  40.7 us
    reshape x2, local copies, waits for them, and re-layouts, shards(): pieces = pieces.reshape(n_own, half, 2 * piece_rows * width_part)  13.7 us
    dot_general x2, matrix products, shards(): jnp.einsum('kcs,kcw->ksw', sig_part, back_pre, preferred_element_type=jnp...  11 us
    reshape x2, local copies, waits for them, and re-layouts, shards(): arrived = arrived.reshape(n_own, half, 2, piece_rows, width_part)  10.6 us
    all_to_all x2, starting transfers between devices, shards(): lax.all_to_all(pieces, 'own', split_axis=0, concat_axis=0, tiled=True)  9.81 us
    transpose x2, local copies, waits for them, and re-layouts, shards(): arrived.transpose(1, 2, 0, 3, 4).reshape(half, 2, SITES, width_part)  8.62 us
  transfers between devices with their start and end apart: 6, of which 5 were waited for; matrix products, arithmetic and copies ran while one was open for 28% of the time, Pallas kernels for 0%

profile of v4, /device:TPU:1, one launch (start us, length us, event | category | flops | bytes accessed | tf_op | source)
XLA Modules:
  0.0 297.5 jit_solution(86080646353261684)
XLA Ops:
  11.4 3.1 %scatter_custom_fusion = bf16[512,768]{1,0:T(8,128)(2,1)} fusion(s32[256]{0:T(256)S(1)} %bitcast.94, bf16[256,384]{1,0:T(8,128)(2,1)} %param.9, bf16[]{:T(256)} %constant.68, bf16[256,384]{1,0:T(8,128)(2,1)} %param.8, bf16[]{:T(256)} %constant.23.clone.1), kind=kCustom, calls=%fused_computation.71 | custom fusion | flops 786432 | bytes 1179652 | tf_op jit(solution)/shard_map/scatter | solution.py:155
  20.6 47.9 %all_to_all.20 = bf16[32,16,3072]{2,1,0:T(8,128)(2,1)} all-to-all(bf16[32,16,3072]{2,1,0:T(8,128)(2,1)S(1)} %get-tuple-element.42), channel_id=1, replica_groups=mesh['dp'=8,'own'=32] {'own'}, dimensions={0} | all-to-all | bytes 6291456 | tf_op jit(solution)/shard_map/all_to_all | solution.py:173
  68.5 4.2 %all-to-all-start.1 = ((bf16[32,16,3072]{2,1,0:T(8,128)(2,1)}), bf16[32,16,3072]{2,1,0:T(8,128)(2,1)S(1)}, u32[]{:S(2)}, u32[]{:S(2)}) async-start(bf16[32,16,3072]{2,1,0:T(8,128)(2,1)} %get-tuple-element.41), calls=%async_computation.1 | async-start | bytes 6291456 | tf_op jit(solution)/shard_map/all_to_all | solution.py:173
  72.7 6.8 %reshape.115 = bf16[32,16,2,12,128]{4,3,2,1,0:T(8,128)(2,1)} reshape(bf16[32,16,3072]{2,1,0:T(8,128)(2,1)} %all_to_all.20) | data formatting | bytes 6291456 | tf_op jit(solution)/shard_map/reshape | solution.py:182
  79.5 4.3 %copy.110 = bf16[16,2,32,12,128]{4,0,3,2,1:T(8,128)(2,1)S(1)} copy(bf16[16,2,32,12,128]{4,3,1,0,2:T(8,128)(2,1)} %bitcast.79) | data formatting | bytes 6291456 | tf_op jit(solution)/shard_map/transpose | solution.py:183
  83.8 2.2 fusion.83
  86.0 6.9 %all-gather.4.cloned.1.call-done = bf16[32,128,768]{2,1,0:T(8,128)(2,1)} async-done(((bf16[4,128,768]{2,1,0:T(8,128)(2,1)}), bf16[32,128,768]{2,1,0:T(8,128)(2,1)}) %all-gather.4.cloned.1.call-update) | async-done | bytes 6291472 | tf_op jit(solution)/shard_map/all_gather | solution.py:157
  92.9 2.7 fusion.1
  95.6 3.8 %fusion.3 = bf16[16,1,384,128]{3,2,0,1:T(8,128)(2,1)} fusion(bf16[32,128,768]{2,1,0:T(8,128)(2,1)} %all-gather.4.cloned.1.call-done, f32[16,128,128]{2,1,0:T(8,128)S(1)} %fusion.1), kind=kOutput, calls=%fused_computation.24 | convolution fusion | flops 204472320 | bytes 4194304 | tf_op jit(solution)/shard_map/kcs,kcw->ksw/dot_general | solution.py:199
  99.5 5.7 %fusion.2 = bf16[16,1,384,128]{3,2,0,1:T(8,128)(2,1)} fusion(bf16[32,128,768]{2,1,0:T(8,128)(2,1)} %all-gather.4.cloned.1.call-done, bf16[16,1,384,128]{3,0,2,1:T(8,128)(2,1)} %get-tuple-element.45, f32[16,128,128]{2,1,0:T(8,128)} %copy-done.12), kind=kOutput, calls=%fused_computation.23 | convolution fusion | flops 408420352 | bytes 7340032 | tf_op jit(solution)/shard_map/kcs,kcw->ksw/dot_general | solution.py:198
  105.2 3.9 %pad_maximum_fusion.1 = bf16[16,2,384,128]{3,2,0,1:T(8,128)(2,1)} fusion(bf16[16,1,384,128]{3,2,0,1:T(8,128)(2,1)} %fusion.3, bf16[16,1,384,128]{3,2,0,1:T(8,128)(2,1)} %fusion.2), kind=kLoop, calls=%fused_computation.6 | loop fusion | flops 1572864 | bytes 6291456 | tf_op jit(solution)/shard_map/stack | solution.py:200
  109.1 3.3 %all-to-all-done.1 = bf16[32,16,3072]{2,1,0:T(8,128)(2,1)S(1)} async-done(((bf16[32,16,3072]{2,1,0:T(8,128)(2,1)}), bf16[32,16,3072]{2,1,0:T(8,128)(2,1)S(1)}, u32[]{:S(2)}, u32[]{:S(2)}) %all-to-all-start.1) | async-done | bytes 3145760 | tf_op jit(solution)/shard_map/all_to_all | solution.py:173
  112.4 3.9 %copy.120 = bf16[16,2,384,128]{3,0,2,1:T(8,128)(2,1)S(1)} copy(bf16[16,2,384,128]{3,2,0,1:T(8,128)(2,1)} %pad_maximum_fusion.1) | data formatting | bytes 6291456 | tf_op jit(solution)/shard_map/optimization_barrier | solution.py:202
  116.3 3.1 %copy.121 = bf16[32,16,2,12,128]{4,3,2,1,0:T(8,128)(2,1)} copy(bf16[32,16,2,12,128]{4,1,3,0,2:T(8,128)(2,1)S(1)} %bitcast.83) | data formatting | bytes 6291456 | tf_op jit(solution)/shard_map/transpose | solution.py:212
  119.4 6.7 %reshape.120 = bf16[32,16,3072]{2,1,0:T(8,128)(2,1)} reshape(bf16[32,16,2,12,128]{4,3,2,1,0:T(8,128)(2,1)} %copy.121) | data formatting | bytes 6291456 | tf_op jit(solution)/shard_map/reshape | solution.py:213
  126.2 4.9 %all-to-all-start.2 = ((bf16[32,16,3072]{2,1,0:T(8,128)(2,1)}), bf16[32,16,3072]{2,1,0:T(8,128)(2,1)}, u32[]{:S(2)}, u32[]{:S(2)}) async-start(bf16[32,16,3072]{2,1,0:T(8,128)(2,1)} %reshape.120), calls=%async_computation.2 | async-start | bytes 6291456 | tf_op jit(solution)/shard_map/all_to_all | solution.py:214
  131.1 3.8 %reshape.117 = bf16[32,16,2,12,128]{4,3,2,1,0:T(8,128)(2,1)} reshape(bf16[32,16,3072]{2,1,0:T(8,128)(2,1)S(1)} %all-to-all-done.1) | data formatting | bytes 6291456 | tf_op jit(solution)/shard_map/reshape | solution.py:182
  135.0 4.4 %copy.115 = bf16[16,2,32,12,128]{4,0,3,2,1:T(8,128)(2,1)S(1)} copy(bf16[16,2,32,12,128]{4,3,1,0,2:T(8,128)(2,1)} %bitcast.80) | data formatting | bytes 6291456 | tf_op jit(solution)/shard_map/transpose | solution.py:183
  140.8 2.8 fusion
  146.7 2.7 fusion.5
  149.4 5.2 %fusion.4 = bf16[16,1,384,128]{3,2,0,1:T(8,128)(2,1)} fusion(bf16[32,128,768]{2,1,0:T(8,128)(2,1)} %all-gather.4.cloned.1.call-done, bf16[16,1,384,128]{3,0,2,1:T(8,128)(2,1)S(1)} %copy-done.5, f32[16,128,128]{2,1,0:T(8,128)} %copy-done.14), kind=kOutput, calls=%fused_computation.25 | convolution fusion | flops 408420352 | bytes 7340032 | tf_op jit(solution)/shard_map/kcs,kcw->ksw/dot_general | solution.py:198
  154.6 3.3 %pad_maximum_fusion.2 = bf16[16,2,384,128]{3,2,0,1:T(8,128)(2,1)} fusion(bf16[16,1,384,128]{3,2,0,1:T(8,128)(2,1)S(1)} %fusion.5, bf16[16,1,384,128]{3,2,0,1:T(8,128)(2,1)} %fusion.4), kind=kLoop, calls=%fused_computation.7 | loop fusion | flops 1572864 | bytes 6291456 | tf_op jit(solution)/shard_map/stack | solution.py:200
  157.9 13.0 %all-to-all-done.2 = bf16[32,16,3072]{2,1,0:T(8,128)(2,1)} async-done(((bf16[32,16,3072]{2,1,0:T(8,128)(2,1)}), bf16[32,16,3072]{2,1,0:T(8,128)(2,1)}, u32[]{:S(2)}, u32[]{:S(2)}) %all-to-all-start.2) | async-done | bytes 3145760 | tf_op jit(solution)/shard_map/all_to_all | solution.py:214
  171.0 3.9 %copy.122 = bf16[16,2,384,128]{3,0,2,1:T(8,128)(2,1)S(1)} copy(bf16[16,2,384,128]{3,2,0,1:T(8,128)(2,1)} %pad_maximum_fusion.2) | data formatting | bytes 6291456 | tf_op jit(solution)/shard_map/optimization_barrier | solution.py:208
  174.9 3.0 %copy.123 = bf16[32,16,2,12,128]{4,3,2,1,0:T(8,128)(2,1)} copy(bf16[32,16,2,12,128]{4,1,3,0,2:T(8,128)(2,1)S(1)} %bitcast.84) | data formatting | bytes 6291456 | tf_op jit(solution)/shard_map/transpose | solution.py:212
  177.9 7.0 %reshape.122 = bf16[32,16,3072]{2,1,0:T(8,128)(2,1)} reshape(bf16[32,16,2,12,128]{4,3,2,1,0:T(8,128)(2,1)} %copy.123) | data formatting | bytes 6291456 | tf_op jit(solution)/shard_map/reshape | solution.py:213
  184.9 4.9 %all-to-all-start.3 = ((bf16[32,16,3072]{2,1,0:T(8,128)(2,1)}), bf16[32,16,3072]{2,1,0:T(8,128)(2,1)S(1)}, u32[]{:S(2)}, u32[]{:S(2)}) async-start(bf16[32,16,3072]{2,1,0:T(8,128)(2,1)} %reshape.122), calls=%async_computation.3 | async-start | bytes 6291456 | tf_op jit(solution)/shard_map/all_to_all | solution.py:214
  193.4 36.2 %all-to-all-done.3 = bf16[32,16,3072]{2,1,0:T(8,128)(2,1)S(1)} async-done(((bf16[32,16,3072]{2,1,0:T(8,128)(2,1)}), bf16[32,16,3072]{2,1,0:T(8,128)(2,1)S(1)}, u32[]{:S(2)}, u32[]{:S(2)}) %all-to-all-start.3) | async-done | bytes 3145760 | tf_op jit(solution)/shard_map/all_to_all | solution.py:214
  231.0 2.5 convolution_add_fusion
  234.7 2.4 subtract_convert_fusion
  242.7 40.7 %all-gather.6.cloned.1.call-done = bf16[512,2,12,128]{3,1,2,0:T(2,128)(2,1)} async-done(((bf16[64,2,12,128]{3,1,2,0:T(2,128)(2,1)}), bf16[512,2,12,128]{3,1,2,0:T(2,128)(2,1)}) %all-gather.6.cloned.1.call-update) | async-done | bytes 3145744 | tf_op jit(solution)/shard_map/all_gather | solution.py:225
  283.4 7.2 %copy.177 = bf16[8,64,12,1,2,128]{5,4,0,3,2,1:T(2,128)(2,1)} copy(bf16[8,64,12,1,2,128]{5,4,3,2,1,0:T(2,128)(2,1)} %bitcast.87) | data formatting | bytes 6291456 | tf_op jit(solution)/shard_map/reshape | solution.py:226
  (75 shorter events, 26.4 us)
Async XLA Ops:
  7.2 8.4 %copy-start = (bf16[64,2,12,1024]{3,1,2,0:T(2,128)(2,1)S(1)}, bf16[64,2,12,1024]{3,1,2,0:T(2,128)(2,1)}, u32[]{:S(2)}) copy-start(bf16[64,2,12,1024]{3,1,2,0:T(2,128)(2,1)} %param.13) | copy-start | bytes 9437188
  7.2 7.3 %copy-start.7 = (s32[256,4]{0,1:T(4,128)S(1)}, s32[256,4]{0,1:T(4,128)}, u32[]{:S(2)}) copy-start(s32[256,4]{0,1:T(4,128)} %param.11) | copy-start | bytes 12292
  7.2 7.3 %copy-start.11 = (s32[64]{0:T(128)S(1)}, s32[64]{0:T(128)}, u32[]{:S(2)}) copy-start(s32[64]{0:T(128)} %param.12) | copy-start | bytes 772
  7.2 85.7 %all-gather.4.cloned.1.call-start = ((), (), s32[]{:S(2)}) async-start(), calls=%async_computation.5 | async-start | bytes 7077888 | tf_op jit(solution)/shard_map/all_gather | solution.py:157
  11.4 3.1 %copy-start.9 = (s32[256,1]{0,1:T(1,128)}, s32[256,1]{0,1:T(1,128)S(1)}, u32[]{:S(2)}) copy-start(s32[256,1]{0,1:T(1,128)S(1)} %compare_select_fusion) | copy-start | bytes 3076
  15.9 0.7 copy-start.6
  68.5 43.9 %all-to-all-start.1 = ((bf16[32,16,3072]{2,1,0:T(8,128)(2,1)}), bf16[32,16,3072]{2,1,0:T(8,128)(2,1)S(1)}, u32[]{:S(2)}, u32[]{:S(2)}) async-start(bf16[32,16,3072]{2,1,0:T(8,128)(2,1)} %get-tuple-element.41), calls=%async_computation.1 | async-start | bytes 6291456 | tf_op jit(solution)/shard_map/all_to_all | solution.py:173
  95.6 3.8 %copy-start.12 = (f32[16,128,128]{2,1,0:T(8,128)}, f32[16,128,128]{2,1,0:T(8,128)S(1)}, u32[]{:S(2)}) copy-start(f32[16,128,128]{2,1,0:T(8,128)S(1)} %fusion.1) | copy-start | bytes 3145732
  126.2 44.8 %all-to-all-start.2 = ((bf16[32,16,3072]{2,1,0:T(8,128)(2,1)}), bf16[32,16,3072]{2,1,0:T(8,128)(2,1)}, u32[]{:S(2)}, u32[]{:S(2)}) async-start(bf16[32,16,3072]{2,1,0:T(8,128)(2,1)} %reshape.120), calls=%async_computation.2 | async-start | bytes 6291456 | tf_op jit(solution)/shard_map/all_to_all | solution.py:214
  131.1 98.5 %reduce-scatter.2.cloned.1.call-start = ((), (), s32[]{:S(2)}) async-start(), calls=%async_computation.6 | async-start | bytes 3538944 | tf_op jit(solution)/shard_map/reduce_scatter | solution.py:209
  134.9 4.4 %copy-start.3 = (bf16[16,1,384,128]{3,0,2,1:T(8,128)(2,1)S(1)}, bf16[16,1,384,128]{3,0,2,1:T(8,128)(2,1)}, u32[]{:S(2)}) copy-start(bf16[16,1,384,128]{3,0,2,1:T(8,128)(2,1)} %get-tuple-element.45) | copy-start | bytes 4718596
  135.0 4.4 %copy-start.13 = (f32[16,128,128]{2,1,0:T(8,128)S(1)}, f32[16,128,128]{2,1,0:T(8,128)}, u32[]{:S(2)}) copy-start(f32[16,128,128]{2,1,0:T(8,128)} %copy-done.12) | copy-start | bytes 3145732
  140.8 2.8 copy-start.4
  143.6 1.1 copy-start.14
  146.7 2.7 copy-start.5
  184.9 44.7 %all-to-all-start.3 = ((bf16[32,16,3072]{2,1,0:T(8,128)(2,1)}), bf16[32,16,3072]{2,1,0:T(8,128)(2,1)S(1)}, u32[]{:S(2)}, u32[]{:S(2)}) async-start(bf16[32,16,3072]{2,1,0:T(8,128)(2,1)} %reshape.122), calls=%async_computation.3 | async-start | bytes 6291456 | tf_op jit(solution)/shard_map/all_to_all | solution.py:214
  189.8 93.5 %all-gather.6.cloned.1.call-start = ((), (), s32[]{:S(2)}) async-start(), calls=%async_computation.7 | async-start | bytes 3538944 | tf_op jit(solution)/shard_map/all_gather | solution.py:225
  229.6 1.4 copy-start.8
  234.7 3.5 %copy-start.10 = (s32[256,1]{0,1:T(1,128)S(1)}, s32[256,1]{0,1:T(1,128)}, u32[]{:S(2)}) copy-start(s32[256,1]{0,1:T(1,128)} %copy-done.9) | copy-start | bytes 3076
  238.3 2.6 copy-start.2
  283.4 7.2 %copy-start.1 = (bf16[64,2,12,1024]{3,1,2,0:T(2,128)(2,1)S(1)}, bf16[64,2,12,1024]{3,1,2,0:T(2,128)(2,1)}, u32[]{:S(2)}) copy-start(bf16[64,2,12,1024]{3,1,2,0:T(2,128)(2,1)} %param.13) | copy-start | bytes 9437188
Sparse Core Ops, SparseCore 0:
  14.6 78.2 all-gather.3
  171.1 44.2 reduce-scatter.1
  238.4 44.9 all-gather.5

commit v5 on v1

--- a/solution.py
+++ b/solution.py
@@ -149,6 +149,7 @@
     peer_rows = stored.reshape(n_dp, n_own, TOUCH).transpose(1, 0, 2).reshape(-1)
     my_list = lax.dynamic_index_in_dim(touched, dp_at * n_own + own_at, 0, keepdims=False)
     places = dispatch(row_insertion, my_list)
+    peer_places = lax.all_gather(places, "dp", axis=0, tiled=False)
     stacked = (
         jnp.zeros((TOUCH * CAP, 2 * SITES), signals.dtype)
         .at[places]
@@ -206,7 +207,9 @@
         if h == halves - 1:
             pred_part = jnp.concatenate(pred_parts, axis=0)
             pred_part, grads = lax.optimization_barrier((pred_part, grads))
-            pred_slots = lax.psum_scatter(pred_part, "dp", scatter_dimension=0, tiled=True)
+            pred_part = pred_part.reshape(n_dp, TOUCH * CAP, SITES)
+            real_rows = jnp.take_along_axis(pred_part, peer_places[:, :, None], axis=1)
+            pred_slots = lax.psum_scatter(real_rows, "dp", scatter_dimension=0, tiled=True)
         pieces = grads.reshape(half, 2, n_own, piece_rows, width_part).transpose(2, 0, 1, 3, 4)
         pieces = pieces.reshape(n_own, half, 2 * piece_rows * width_part)
         arrived_grad = lax.all_to_all(pieces, "own", split_axis=0, concat_axis=0, tiled=True)
@@ -222,7 +225,7 @@
     fresh_part, new_moment1, new_moment2 = adam_step(own_params, moment1, moment2, table)
     new_weights = lax.all_gather(fresh_part, "dp", axis=0, tiled=False)
     new_weights = new_weights.transpose(1, 2, 3, 0, 4).reshape(weights.shape)
-    predicted = pred_slots.reshape(TOUCH * CAP, SITES)[places]
+    predicted = pred_slots.reshape(-1, SITES)
     return (predicted, new_weights, new_moment1, new_moment2)
 
 

time: 316 us -> 349 us (1.10)
  local copies, waits for them, and re-layouts: 74.3 us -> 108 us
  waiting for transfers between devices: 111 us -> 79.3 us
  blocking collectives: 47.9 us -> 66.1 us
  other arithmetic: 18.9 us -> 23.2 us
  starting transfers between devices: 15 us -> 19.1 us
    gather x1, local copies, waits for them, and re-layouts: 1.82 us -> 34.1 us  [shards(): real_rows = jnp.take_along_axis(pred_part, peer_places[:, :, None], axis=1)]
    all_gather x0 -> x1, blocking collectives: none -> 18.2 us  [shards(): peer_places = lax.all_gather(places, 'dp', axis=0, tiled=False)]
    reduce_scatter x1, waiting for transfers between devices: 16.2 us -> 0.01 us  [shards(): lax.psum_scatter(real_rows, 'dp', scatter_dimension=0, tiled=True)]
    all_gather x1, waiting for transfers between devices: 7.57 us -> 0.01 us  [shards(): lax.all_gather(stacked.reshape(TOUCH, CAP, 2 * SITES), 'dp', axis=0, tile...]
    all_to_all x2, starting transfers between devices: 10.3 us -> 14.8 us  [shards(): lax.all_to_all(pieces, 'own', split_axis=0, concat_axis=0, tiled=True)]
    all_to_all x2, waiting for transfers between devices: 46 us -> 42.4 us  [shards(): lax.all_to_all(pieces, 'own', split_axis=0, concat_axis=0, tiled=True)]
  transfers between devices with their start and end apart: 6 -> 6, of which waited for: 6 -> 3; matrix products, arithmetic and copies ran while one was open for 27% -> 26% of each run, Pallas kernels for 0% -> 0%
where the time goes in v5:
time: 349 us; the launch traced here: 342 us
  local copies, waits for them, and re-layouts  108 us (31%)
  waiting for transfers between devices  79.3 us (23%)
  blocking collectives  66.1 us (19%)
  matrix products  32.4 us (9%)
  other arithmetic  23.2 us (7%)
  starting transfers between devices  19.1 us (5%)
  between operations  14.3 us (4%)
    all_to_all x1, blocking collectives, shards(): lax.all_to_all(outgoing[:, h * half:(h + 1) * half], 'own', split_axis=0,...  47.9 us
    all_to_all x2, waiting for transfers between devices, shards(): lax.all_to_all(pieces, 'own', split_axis=0, concat_axis=0, tiled=True)  42.4 us
    all_gather x1, waiting for transfers between devices, shards(): new_weights = lax.all_gather(fresh_part, 'dp', axis=0, tiled=False)  36.8 us
    gather x1, local copies, waits for them, and re-layouts, shards(): real_rows = jnp.take_along_axis(pred_part, peer_places[:, :, None], axis=1)  34.1 us
    all_gather x1, blocking collectives, shards(): peer_places = lax.all_gather(places, 'dp', axis=0, tiled=False)  18.2 us
    all_to_all x2, starting transfers between devices, shards(): lax.all_to_all(pieces, 'own', split_axis=0, concat_axis=0, tiled=True)  14.8 us
    reshape x2, local copies, waits for them, and re-layouts, shards(): arrived = arrived.reshape(n_own, half, 2, piece_rows, width_part)  13.6 us
    reshape x2, local copies, waits for them, and re-layouts, shards(): pieces = pieces.reshape(n_own, half, 2 * piece_rows * width_part)  13.5 us
  transfers between devices with their start and end apart: 6, of which 3 were waited for; matrix products, arithmetic and copies ran while one was open for 26% of the time, Pallas kernels for 0%

profile of v5, /device:TPU:1, one launch (start us, length us, event | category | flops | bytes accessed | tf_op | source)
XLA Modules:
  0.0 342.3 jit_solution(9295648391207284104)
XLA Ops:
  12.0 3.1 scatter_custom_fusion
  20.2 47.9 %all_to_all.20 = bf16[32,16,3072]{2,1,0:T(8,128)(2,1)} all-to-all(bf16[32,16,3072]{2,1,0:T(8,128)(2,1)S(1)} %get-tuple-element.42), channel_id=1, replica_groups=mesh['dp'=8,'own'=32] {'own'}, dimensions={0} | all-to-all | bytes 6291456 | tf_op jit(solution)/shard_map/all_to_all | solution.py:174
  68.1 4.0 %all-to-all-start.1 = ((bf16[32,16,3072]{2,1,0:T(8,128)(2,1)}), bf16[32,16,3072]{2,1,0:T(8,128)(2,1)S(1)}, u32[]{:S(2)}, u32[]{:S(2)}) async-start(bf16[32,16,3072]{2,1,0:T(8,128)(2,1)} %get-tuple-element.41), calls=%async_computation.1 | async-start | bytes 6291456 | tf_op jit(solution)/shard_map/all_to_all | solution.py:174
  72.1 18.2 %all-gather.2 = s32[8,1,256]{2,1,0:T(1,128)} all-gather(s32[1,1,256]{2,1,0:T(1,128)} %bitcast.113), channel_id=2, replica_groups=mesh['dp'=8,'own'=32] {'dp'}, dimensions={0}, use_global_device_ids=true | all-gather | bytes 9216 | tf_op jit(solution)/shard_map/all_gather | solution.py:152
  90.2 6.8 %reshape.143 = bf16[32,16,2,12,128]{4,3,2,1,0:T(8,128)(2,1)} reshape(bf16[32,16,3072]{2,1,0:T(8,128)(2,1)} %all_to_all.20) | data formatting | bytes 6291456 | tf_op jit(solution)/shard_map/reshape | solution.py:183
  97.0 4.2 %copy.110 = bf16[16,2,32,12,128]{4,0,3,2,1:T(8,128)(2,1)S(1)} copy(bf16[16,2,32,12,128]{4,3,1,0,2:T(8,128)(2,1)} %bitcast.98) | data formatting | bytes 6291456 | tf_op jit(solution)/shard_map/transpose | solution.py:184
  103.5 2.7 fusion.1
  107.2 3.5 %fusion.3 = bf16[16,1,384,128]{3,2,0,1:T(8,128)(2,1)} fusion(bf16[32,128,768]{2,1,0:T(8,128)(2,1)} %all-gather.6.cloned.1.call-done, f32[16,128,128]{2,1,0:T(8,128)S(1)} %fusion.1), kind=kOutput, calls=%fused_computation.25 | convolution fusion | flops 204472320 | bytes 4194304 | tf_op jit(solution)/shard_map/kcs,kcw->ksw/dot_general | solution.py:200
  110.7 5.7 %fusion.2 = bf16[16,1,384,128]{3,2,0,1:T(8,128)(2,1)} fusion(bf16[32,128,768]{2,1,0:T(8,128)(2,1)} %all-gather.6.cloned.1.call-done, bf16[16,1,384,128]{3,0,2,1:T(8,128)(2,1)} %get-tuple-element.45, f32[16,128,128]{2,1,0:T(8,128)} %copy-done.6), kind=kOutput, calls=%fused_computation.24 | convolution fusion | flops 408420352 | bytes 7340032 | tf_op jit(solution)/shard_map/kcs,kcw->ksw/dot_general | solution.py:199
  116.4 3.9 %pad_maximum_fusion.1 = bf16[16,2,384,128]{3,2,0,1:T(8,128)(2,1)} fusion(bf16[16,1,384,128]{3,2,0,1:T(8,128)(2,1)} %fusion.3, bf16[16,1,384,128]{3,2,0,1:T(8,128)(2,1)} %fusion.2), kind=kLoop, calls=%fused_computation.6 | loop fusion | flops 1572864 | bytes 6291456 | tf_op jit(solution)/shard_map/stack | solution.py:201
  120.3 5.1 %copy.120 = bf16[16,2,384,128]{3,0,2,1:T(8,128)(2,1)S(1)} copy(bf16[16,2,384,128]{3,2,0,1:T(8,128)(2,1)} %pad_maximum_fusion.1) | data formatting | bytes 6291456 | tf_op jit(solution)/shard_map/optimization_barrier | solution.py:203
  125.4 3.1 copy.121
  128.5 6.8 %reshape.148 = bf16[32,16,3072]{2,1,0:T(8,128)(2,1)} reshape(bf16[32,16,2,12,128]{4,3,2,1,0:T(8,128)(2,1)} %copy.121) | data formatting | bytes 6291456 | tf_op jit(solution)/shard_map/reshape | solution.py:214
  135.2 9.7 %all-to-all-start.2 = ((bf16[32,16,3072]{2,1,0:T(8,128)(2,1)}), bf16[32,16,3072]{2,1,0:T(8,128)(2,1)}, u32[]{:S(2)}, u32[]{:S(2)}) async-start(bf16[32,16,3072]{2,1,0:T(8,128)(2,1)} %reshape.148), calls=%async_computation.2 | async-start | bytes 6291456 | tf_op jit(solution)/shard_map/all_to_all | solution.py:215
  145.2 6.8 %reshape.145 = bf16[32,16,2,12,128]{4,3,2,1,0:T(8,128)(2,1)} reshape(bf16[32,16,3072]{2,1,0:T(8,128)(2,1)} %copy-done.2) | data formatting | bytes 6291456 | tf_op jit(solution)/shard_map/reshape | solution.py:183
  152.0 4.2 %copy.115 = bf16[16,2,32,12,128]{4,0,3,2,1:T(8,128)(2,1)S(1)} copy(bf16[16,2,32,12,128]{4,3,1,0,2:T(8,128)(2,1)} %bitcast.99) | data formatting | bytes 6291456 | tf_op jit(solution)/shard_map/transpose | solution.py:184
  156.8 2.8 fusion
  159.6 3.8 %fusion.5 = bf16[16,1,384,128]{3,2,0,1:T(8,128)(2,1)} fusion(bf16[32,128,768]{2,1,0:T(8,128)(2,1)} %all-gather.6.cloned.1.call-done, f32[16,128,128]{2,1,0:T(8,128)S(1)} %fusion), kind=kOutput, calls=%fused_computation.27 | convolution fusion | flops 204472320 | bytes 4194304 | tf_op jit(solution)/shard_map/kcs,kcw->ksw/dot_general | solution.py:200
  163.4 5.0 %fusion.4 = bf16[16,1,384,128]{3,2,0,1:T(8,128)(2,1)} fusion(bf16[32,128,768]{2,1,0:T(8,128)(2,1)} %all-gather.6.cloned.1.call-done, bf16[16,1,384,128]{3,0,2,1:T(8,128)(2,1)S(1)} %get-tuple-element.44, f32[16,128,128]{2,1,0:T(8,128)S(1)} %fusion), kind=kOutput, calls=%fused_computation.26 | convolution fusion | flops 408420352 | bytes 7340032 | tf_op jit(solution)/shard_map/kcs,kcw->ksw/dot_general | solution.py:199
  168.4 3.9 %pad_maximum_fusion.2 = bf16[16,2,384,128]{3,2,0,1:T(8,128)(2,1)} fusion(bf16[16,1,384,128]{3,2,0,1:T(8,128)(2,1)} %fusion.5, bf16[16,1,384,128]{3,2,0,1:T(8,128)(2,1)} %fusion.4), kind=kLoop, calls=%fused_computation.7 | loop fusion | flops 1572864 | bytes 6291456 | tf_op jit(solution)/shard_map/stack | solution.py:201
  175.5 3.0 pad_maximum_fusion
  178.6 6.2 %all-to-all-done.2 = bf16[32,16,3072]{2,1,0:T(8,128)(2,1)} async-done(((bf16[32,16,3072]{2,1,0:T(8,128)(2,1)}), bf16[32,16,3072]{2,1,0:T(8,128)(2,1)}, u32[]{:S(2)}, u32[]{:S(2)}) %all-to-all-start.2) | async-done | bytes 3145760 | tf_op jit(solution)/shard_map/all_to_all | solution.py:215
  184.8 34.1 %gather_fusion = f32[2048,384]{1,0:T(8,128)} fusion(f32[8,512,384]{2,1,0:T(8,128)} %bitcast.95, s32[2048]{0:T(1024)S(1)} %bitcast.96), kind=kCustom, calls=%fused_computation | custom fusion | bytes 6307840 | tf_op jit(solution)/shard_map/jit(take_along_axis)/gather | solution.py:211
  218.8 3.5 %broadcast_select_fusion = f32[8,256,384]{2,1,0:T(8,128)} fusion(f32[8,256,384]{2,1,0:T(8,128)} %bitcast.102, pred[8,256]{1,0:T(8,128)(4,1)S(1)} %compare_and_fusion), kind=kLoop, calls=%fused_computation.19 | loop fusion | flops 786432 | bytes 6293504 | tf_op jit(solution)/shard_map/jit(take_along_axis)/select_n | solution.py:211
  222.3 3.9 %copy.122 = bf16[16,2,384,128]{3,0,2,1:T(8,128)(2,1)S(1)} copy(bf16[16,2,384,128]{3,2,0,1:T(8,128)(2,1)} %pad_maximum_fusion.2) | data formatting | bytes 6291456 | tf_op jit(solution)/shard_map/optimization_barrier | solution.py:209
  226.2 3.1 copy.123
  229.3 6.8 %reshape.150 = bf16[32,16,3072]{2,1,0:T(8,128)(2,1)} reshape(bf16[32,16,2,12,128]{4,3,2,1,0:T(8,128)(2,1)} %copy.123) | data formatting | bytes 6291456 | tf_op jit(solution)/shard_map/reshape | solution.py:214
  236.1 5.1 %all-to-all-start.3 = ((bf16[32,16,3072]{2,1,0:T(8,128)(2,1)}), bf16[32,16,3072]{2,1,0:T(8,128)(2,1)S(1)}, u32[]{:S(2)}, u32[]{:S(2)}) async-start(bf16[32,16,3072]{2,1,0:T(8,128)(2,1)} %reshape.150), calls=%async_computation.3 | async-start | bytes 6291456 | tf_op jit(solution)/shard_map/all_to_all | solution.py:215
  244.7 36.2 %all-to-all-done.3 = bf16[32,16,3072]{2,1,0:T(8,128)(2,1)S(1)} async-done(((bf16[32,16,3072]{2,1,0:T(8,128)(2,1)}), bf16[32,16,3072]{2,1,0:T(8,128)(2,1)S(1)}, u32[]{:S(2)}, u32[]{:S(2)}) %all-to-all-start.3) | async-done | bytes 3145760 | tf_op jit(solution)/shard_map/all_to_all | solution.py:215
  282.3 2.5 convolution_add_fusion
  291.6 36.8 %all-gather.8.cloned.1.call-done = bf16[512,2,12,128]{3,1,2,0:T(2,128)(2,1)} async-done(((bf16[64,2,12,128]{3,1,2,0:T(2,128)(2,1)}), bf16[512,2,12,128]{3,1,2,0:T(2,128)(2,1)}) %all-gather.8.cloned.1.call-update) | async-done | bytes 3145744 | tf_op jit(solution)/shard_map/all_gather | solution.py:226
  328.4 7.2 %copy.184 = bf16[8,64,12,1,2,128]{5,4,0,3,2,1:T(2,128)(2,1)} copy(bf16[8,64,12,1,2,128]{5,4,3,2,1,0:T(2,128)(2,1)} %bitcast.106) | data formatting | bytes 6291456 | tf_op jit(solution)/shard_map/reshape | solution.py:227
  (80 shorter events, 28.7 us)
Async XLA Ops:
  7.2 7.9 %copy-start = (bf16[64,2,12,1024]{3,1,2,0:T(2,128)(2,1)S(1)}, bf16[64,2,12,1024]{3,1,2,0:T(2,128)(2,1)}, u32[]{:S(2)}) copy-start(bf16[64,2,12,1024]{3,1,2,0:T(2,128)(2,1)} %param.13) | copy-start | bytes 9437188
  7.2 8.6 %copy-start.12 = (s32[256,4]{0,1:T(4,128)S(1)}, s32[256,4]{0,1:T(4,128)}, u32[]{:S(2)}) copy-start(s32[256,4]{0,1:T(4,128)} %param.11) | copy-start | bytes 12292
  7.2 8.6 %copy-start.14 = (s32[64]{0:T(128)S(1)}, s32[64]{0:T(128)}, u32[]{:S(2)}) copy-start(s32[64]{0:T(128)} %param.12) | copy-start | bytes 772
  7.2 96.3 %all-gather.6.cloned.1.call-start = ((), (), s32[]{:S(2)}) async-start(), calls=%async_computation.5 | async-start | bytes 7077888 | tf_op jit(solution)/shard_map/all_gather | solution.py:158
  11.4 0.6 copy-start.11
  68.1 52.2 %all-to-all-start.1 = ((bf16[32,16,3072]{2,1,0:T(8,128)(2,1)}), bf16[32,16,3072]{2,1,0:T(8,128)(2,1)S(1)}, u32[]{:S(2)}, u32[]{:S(2)}) async-start(bf16[32,16,3072]{2,1,0:T(8,128)(2,1)} %get-tuple-element.41), calls=%async_computation.1 | async-start | bytes 6291456 | tf_op jit(solution)/shard_map/all_to_all | solution.py:174
  106.2 1.0 copy-start.6
  120.3 5.1 %copy-start.2 = (bf16[32,16,3072]{2,1,0:T(8,128)(2,1)}, bf16[32,16,3072]{2,1,0:T(8,128)(2,1)S(1)}, u32[]{:S(2)}) copy-start(bf16[32,16,3072]{2,1,0:T(8,128)(2,1)S(1)} %all-to-all-done.1) | copy-start | bytes 9437188
  135.2 9.9 %copy-start.10 = (s32[8,1,256]{2,1,0:T(1,128)S(1)}, s32[8,1,256]{2,1,0:T(1,128)}, u32[]{:S(2)}) copy-start(s32[8,1,256]{2,1,0:T(1,128)} %all-gather.2) | copy-start | bytes 24580
  135.2 49.5 %all-to-all-start.2 = ((bf16[32,16,3072]{2,1,0:T(8,128)(2,1)}), bf16[32,16,3072]{2,1,0:T(8,128)(2,1)}, u32[]{:S(2)}, u32[]{:S(2)}) async-start(bf16[32,16,3072]{2,1,0:T(8,128)(2,1)} %reshape.148), calls=%async_computation.2 | async-start | bytes 6291456 | tf_op jit(solution)/shard_map/all_to_all | solution.py:215
  144.9 136.0 %reduce-scatter.2.cloned.1.call-start = ((), (), s32[]{:S(2)}) async-start(), calls=%async_computation.6 | async-start | bytes 3538944 | tf_op jit(solution)/shard_map/reduce_scatter | solution.py:212
  156.8 6.6 %copy-start.4 = (bf16[16,1,384,128]{3,0,2,1:T(8,128)(2,1)}, bf16[16,1,384,128]{3,0,2,1:T(8,128)(2,1)S(1)}, u32[]{:S(2)}) copy-start(bf16[16,1,384,128]{3,0,2,1:T(8,128)(2,1)S(1)} %get-tuple-element.44) | copy-start | bytes 4718596
  159.6 8.8 %copy-start.8 = (f32[16,128,128]{2,1,0:T(8,128)}, f32[16,128,128]{2,1,0:T(8,128)S(1)}, u32[]{:S(2)}) copy-start(f32[16,128,128]{2,1,0:T(8,128)S(1)} %fusion) | copy-start | bytes 3145732
  168.4 3.9 %copy-start.5 = (bf16[16,1,384,128]{3,0,2,1:T(8,128)(2,1)S(1)}, bf16[16,1,384,128]{3,0,2,1:T(8,128)(2,1)}, u32[]{:S(2)}) copy-start(bf16[16,1,384,128]{3,0,2,1:T(8,128)(2,1)} %copy-done.4) | copy-start | bytes 4718596
  172.3 2.3 copy-start.3
  172.3 2.3 copy-start.7
  236.1 44.9 %all-to-all-start.3 = ((bf16[32,16,3072]{2,1,0:T(8,128)(2,1)}), bf16[32,16,3072]{2,1,0:T(8,128)(2,1)S(1)}, u32[]{:S(2)}, u32[]{:S(2)}) async-start(bf16[32,16,3072]{2,1,0:T(8,128)(2,1)} %reshape.150), calls=%async_computation.3 | async-start | bytes 6291456 | tf_op jit(solution)/shard_map/all_to_all | solution.py:215
  241.2 87.2 %all-gather.8.cloned.1.call-start = ((), (), s32[]{:S(2)}) async-start(), calls=%async_computation.7 | async-start | bytes 3538944 | tf_op jit(solution)/shard_map/all_gather | solution.py:226
  244.7 37.6 %copy-start.13 = (s32[512]{0:T(512)S(1)}, s32[512]{0:T(512)}, u32[]{:S(2)}) copy-start(s32[512]{0:T(512)} %eq.103) | copy-start | bytes 6148
  287.2 3.7 %copy-start.9 = (f32[1,256,384]{2,1,0:T(8,128)S(1)}, f32[1,256,384]{2,1,0:T(8,128)}, u32[]{:S(2)}) copy-start(f32[1,256,384]{2,1,0:T(8,128)} %reduce-scatter.2.cloned.1.call-done) | copy-start | bytes 1179652
  328.4 7.2 %copy-start.1 = (bf16[64,2,12,1024]{3,1,2,0:T(2,128)(2,1)S(1)}, bf16[64,2,12,1024]{3,1,2,0:T(2,128)(2,1)}, u32[]{:S(2)}) copy-start(bf16[64,2,12,1024]{3,1,2,0:T(2,128)(2,1)} %param.13) | copy-start | bytes 9437188
Sparse Core Ops, SparseCore 0:
  15.2 78.3 all-gather.5
  222.4 39.5 reduce-scatter.1
  288.4 39.9 all-gather.7

commit v6 on v1

--- a/solution.py
+++ b/solution.py
@@ -220,8 +220,8 @@
     table = table.reshape(number, 2, piece_rows, width_part)
     own_params = my_width.astype(jnp.float32)
     fresh_part, new_moment1, new_moment2 = adam_step(own_params, moment1, moment2, table)
-    new_weights = lax.all_gather(fresh_part, "dp", axis=0, tiled=False)
-    new_weights = new_weights.transpose(1, 2, 3, 0, 4).reshape(weights.shape)
+    new_weights = lax.all_gather(fresh_part.reshape(-1, width_part), "dp", axis=0, tiled=False)
+    new_weights = new_weights.transpose(1, 0, 2).reshape(weights.shape)
     predicted = pred_slots.reshape(TOUCH * CAP, SITES)[places]
     return (predicted, new_weights, new_moment1, new_moment2)
 

time: 316 us -> 336 us (1.063)
  local copies, waits for them, and re-layouts: 74.3 us -> 92.9 us
    transpose x0 -> x1, local copies, waits for them, and re-layouts: none -> 10.7 us  [shards(): new_weights = new_weights.transpose(1, 0, 2).reshape(weights.shape)]
    unnamed x33 -> x34, local copies, waits for them, and re-layouts: 5.39 us -> 12.6 us
  transfers between devices with their start and end apart: 6 -> 6, of which waited for: 6 -> 6; matrix products, arithmetic and copies ran while one was open for 27% -> 26% of each run, Pallas kernels for 0% -> 0%
where the time goes in v6:
time: 336 us; the launch traced here: 330 us
  waiting for transfers between devices  111 us (33%)
  local copies, waits for them, and re-layouts  92.9 us (28%)
  blocking collectives  47.9 us (14%)
  matrix products  29.3 us (9%)
  other arithmetic  19.7 us (6%)
  starting transfers between devices  15 us (4%)
  between operations  14.3 us (4%)
    all_to_all x1, blocking collectives, shards(): lax.all_to_all(outgoing[:, h * half:(h + 1) * half], 'own', split_axis=0,...  47.9 us
    all_to_all x2, waiting for transfers between devices, shards(): lax.all_to_all(pieces, 'own', split_axis=0, concat_axis=0, tiled=True)  46 us
    all_gather x1, waiting for transfers between devices, shards(): lax.all_gather(fresh_part.reshape(-1, width_part), 'dp', axis=0, tiled=Fa...  39 us
    reduce_scatter x1, waiting for transfers between devices, shards(): lax.psum_scatter(pred_part, 'dp', scatter_dimension=0, tiled=True)  16.2 us
    reshape x2, local copies, waits for them, and re-layouts, shards(): pieces = pieces.reshape(n_own, half, 2 * piece_rows * width_part)  13.8 us
    unnamed x34, local copies, waits for them, and re-layouts  12.6 us
    dot_general x2, matrix products, shards(): jnp.einsum('kcs,kcw->ksw', sig_part, back_pre, preferred_element_type=jnp...  11.1 us
    transpose x1, local copies, waits for them, and re-layouts, shards(): new_weights = new_weights.transpose(1, 0, 2).reshape(weights.shape)  10.7 us
  transfers between devices with their start and end apart: 6, of which 6 were waited for; matrix products, arithmetic and copies ran while one was open for 26% of the time, Pallas kernels for 0%

profile of v6, /device:TPU:1, one launch (start us, length us, event | category | flops | bytes accessed | tf_op | source)
XLA Modules:
  0.0 329.9 jit_solution(5581954147155757958)
XLA Ops:
  11.4 3.1 scatter_custom_fusion
  19.7 47.9 %all_to_all.20 = bf16[32,16,3072]{2,1,0:T(8,128)(2,1)} all-to-all(bf16[32,16,3072]{2,1,0:T(8,128)(2,1)S(1)} %get-tuple-element.42), channel_id=1, replica_groups=mesh['dp'=8,'own'=32] {'own'}, dimensions={0} | all-to-all | bytes 6291456 | tf_op jit(solution)/shard_map/all_to_all | solution.py:173
  67.6 4.5 %all-to-all-start.1 = ((bf16[32,16,3072]{2,1,0:T(8,128)(2,1)}), bf16[32,16,3072]{2,1,0:T(8,128)(2,1)S(1)}, u32[]{:S(2)}, u32[]{:S(2)}) async-start(bf16[32,16,3072]{2,1,0:T(8,128)(2,1)} %get-tuple-element.41), calls=%async_computation.1 | async-start | bytes 6291456 | tf_op jit(solution)/shard_map/all_to_all | solution.py:173
  72.1 6.8 %reshape.115 = bf16[32,16,2,12,128]{4,3,2,1,0:T(8,128)(2,1)} reshape(bf16[32,16,3072]{2,1,0:T(8,128)(2,1)} %all_to_all.20) | data formatting | bytes 6291456 | tf_op jit(solution)/shard_map/reshape | solution.py:182
  78.9 4.2 %copy.111 = bf16[16,2,32,12,128]{4,0,3,2,1:T(8,128)(2,1)S(1)} copy(bf16[16,2,32,12,128]{4,3,1,0,2:T(8,128)(2,1)} %bitcast.72) | data formatting | bytes 6291456 | tf_op jit(solution)/shard_map/transpose | solution.py:183
  85.4 7.6 %all-gather.3.cloned.1.call-done = bf16[32,128,768]{2,1,0:T(8,128)(2,1)} async-done(((bf16[4,128,768]{2,1,0:T(8,128)(2,1)}), bf16[32,128,768]{2,1,0:T(8,128)(2,1)}) %all-gather.3.cloned.1.call-update) | async-done | bytes 6291472 | tf_op jit(solution)/shard_map/all_gather | solution.py:157
  92.9 2.7 fusion.1
  96.6 3.4 %fusion.3 = bf16[16,1,384,128]{3,2,0,1:T(8,128)(2,1)} fusion(bf16[32,128,768]{2,1,0:T(8,128)(2,1)} %all-gather.3.cloned.1.call-done, f32[16,128,128]{2,1,0:T(8,128)S(1)} %fusion.1), kind=kOutput, calls=%fused_computation.23 | convolution fusion | flops 204472320 | bytes 4194304 | tf_op jit(solution)/shard_map/kcs,kcw->ksw/dot_general | solution.py:199
  100.0 5.7 %fusion.2 = bf16[16,1,384,128]{3,2,0,1:T(8,128)(2,1)} fusion(bf16[32,128,768]{2,1,0:T(8,128)(2,1)} %all-gather.3.cloned.1.call-done, bf16[16,1,384,128]{3,0,2,1:T(8,128)(2,1)} %get-tuple-element.45, f32[16,128,128]{2,1,0:T(8,128)} %copy-done.5), kind=kOutput, calls=%fused_computation.22 | convolution fusion | flops 408420352 | bytes 7340032 | tf_op jit(solution)/shard_map/kcs,kcw->ksw/dot_general | solution.py:198
  105.8 3.9 %pad_maximum_fusion.1 = bf16[16,2,384,128]{3,2,0,1:T(8,128)(2,1)} fusion(bf16[16,1,384,128]{3,2,0,1:T(8,128)(2,1)} %fusion.3, bf16[16,1,384,128]{3,2,0,1:T(8,128)(2,1)} %fusion.2), kind=kLoop, calls=%fused_computation.5 | loop fusion | flops 1572864 | bytes 6291456 | tf_op jit(solution)/shard_map/stack | solution.py:200
  111.8 3.9 %copy.121 = bf16[16,2,384,128]{3,0,2,1:T(8,128)(2,1)S(1)} copy(bf16[16,2,384,128]{3,2,0,1:T(8,128)(2,1)} %pad_maximum_fusion.1) | data formatting | bytes 6291456 | tf_op jit(solution)/shard_map/optimization_barrier | solution.py:202
  115.7 3.1 copy.122
  118.8 6.7 %reshape.120 = bf16[32,16,3072]{2,1,0:T(8,128)(2,1)} reshape(bf16[32,16,2,12,128]{4,3,2,1,0:T(8,128)(2,1)} %copy.122) | data formatting | bytes 6291456 | tf_op jit(solution)/shard_map/reshape | solution.py:211
  125.5 5.5 %all-to-all-start.2 = ((bf16[32,16,3072]{2,1,0:T(8,128)(2,1)}), bf16[32,16,3072]{2,1,0:T(8,128)(2,1)}, u32[]{:S(2)}, u32[]{:S(2)}) async-start(bf16[32,16,3072]{2,1,0:T(8,128)(2,1)} %reshape.120), calls=%async_computation.2 | async-start | bytes 6291456 | tf_op jit(solution)/shard_map/all_to_all | solution.py:212
  131.1 3.8 %reshape.117 = bf16[32,16,2,12,128]{4,3,2,1,0:T(8,128)(2,1)} reshape(bf16[32,16,3072]{2,1,0:T(8,128)(2,1)S(1)} %all-to-all-done.1) | data formatting | bytes 6291456 | tf_op jit(solution)/shard_map/reshape | solution.py:182
  134.9 4.2 %copy.116 = bf16[16,2,32,12,128]{4,0,3,2,1:T(8,128)(2,1)S(1)} copy(bf16[16,2,32,12,128]{4,3,1,0,2:T(8,128)(2,1)} %bitcast.73) | data formatting | bytes 6291456 | tf_op jit(solution)/shard_map/transpose | solution.py:183
  146.4 5.3 %fusion.4 = bf16[16,1,384,128]{3,2,0,1:T(8,128)(2,1)} fusion(bf16[32,128,768]{2,1,0:T(8,128)(2,1)} %all-gather.3.cloned.1.call-done, bf16[16,1,384,128]{3,0,2,1:T(8,128)(2,1)S(1)} %copy-done.3, f32[16,128,128]{2,1,0:T(8,128)} %copy-done.7), kind=kOutput, calls=%fused_computation.24 | convolution fusion | flops 408420352 | bytes 7340032 | tf_op jit(solution)/shard_map/kcs,kcw->ksw/dot_general | solution.py:198
  151.7 3.5 %pad_maximum_fusion.2 = bf16[16,2,384,128]{3,2,0,1:T(8,128)(2,1)} fusion(bf16[16,1,384,128]{3,2,0,1:T(8,128)(2,1)S(1)} %fusion.5, bf16[16,1,384,128]{3,2,0,1:T(8,128)(2,1)} %fusion.4), kind=kLoop, calls=%fused_computation.6 | loop fusion | flops 1572864 | bytes 6291456 | tf_op jit(solution)/shard_map/stack | solution.py:200
  157.8 3.2 pad_maximum_fusion
  161.1 9.8 %all-to-all-done.2 = bf16[32,16,3072]{2,1,0:T(8,128)(2,1)} async-done(((bf16[32,16,3072]{2,1,0:T(8,128)(2,1)}), bf16[32,16,3072]{2,1,0:T(8,128)(2,1)}, u32[]{:S(2)}, u32[]{:S(2)}) %all-to-all-start.2) | async-done | bytes 3145760 | tf_op jit(solution)/shard_map/all_to_all | solution.py:212
  170.9 3.9 %copy.123 = bf16[16,2,384,128]{3,0,2,1:T(8,128)(2,1)S(1)} copy(bf16[16,2,384,128]{3,2,0,1:T(8,128)(2,1)} %pad_maximum_fusion.2) | data formatting | bytes 6291456 | tf_op jit(solution)/shard_map/optimization_barrier | solution.py:208
  174.8 3.1 copy.124
  177.9 7.1 %reshape.122 = bf16[32,16,3072]{2,1,0:T(8,128)(2,1)} reshape(bf16[32,16,2,12,128]{4,3,2,1,0:T(8,128)(2,1)} %copy.124) | data formatting | bytes 6291456 | tf_op jit(solution)/shard_map/reshape | solution.py:211
  185.0 4.9 %all-to-all-start.3 = ((bf16[32,16,3072]{2,1,0:T(8,128)(2,1)}), bf16[32,16,3072]{2,1,0:T(8,128)(2,1)S(1)}, u32[]{:S(2)}, u32[]{:S(2)}) async-start(bf16[32,16,3072]{2,1,0:T(8,128)(2,1)} %reshape.122), calls=%async_computation.3 | async-start | bytes 6291456 | tf_op jit(solution)/shard_map/all_to_all | solution.py:212
  193.4 36.2 %all-to-all-done.3 = bf16[32,16,3072]{2,1,0:T(8,128)(2,1)S(1)} async-done(((bf16[32,16,3072]{2,1,0:T(8,128)(2,1)}), bf16[32,16,3072]{2,1,0:T(8,128)(2,1)S(1)}, u32[]{:S(2)}, u32[]{:S(2)}) %all-to-all-start.3) | async-done | bytes 3145760 | tf_op jit(solution)/shard_map/all_to_all | solution.py:212
  229.6 16.2 %reduce-scatter.2.cloned.1.call-done = f32[4,128,384]{2,1,0:T(8,128)} async-done(((f32[32,128,384]{2,1,0:T(8,128)}), f32[4,128,384]{2,1,0:T(8,128)}) %reduce-scatter.2.cloned.1.call-update) | async-done | bytes 786448 | tf_op jit(solution)/shard_map/reduce_scatter | solution.py:209
  247.2 2.5 convolution_add_fusion
  249.9 2.9 subtract_convert_fusion
  259.3 39.0 %all-gather.5.cloned.1.call-done = bf16[8,1536,128]{2,1,0:T(8,128)(2,1)} async-done(((bf16[1,1536,128]{2,1,0:T(8,128)(2,1)}), bf16[8,1536,128]{2,1,0:T(8,128)(2,1)}) %all-gather.5.cloned.1.call-update) | async-done | bytes 3145744 | tf_op jit(solution)/shard_map/all_gather | solution.py:223
  298.3 10.7 %copy.130 = bf16[1536,8,128]{2,1,0:T(8,128)(2,1)} copy(bf16[1536,8,128]{2,0,1:T(8,128)(2,1)} %bitcast.80) | data formatting | bytes 6291456 | tf_op jit(solution)/shard_map/transpose | solution.py:224
  309.0 7.0 %reshape.127 = bf16[64,2,12,1024]{3,2,1,0:T(8,128)(2,1)} reshape(bf16[1536,8,128]{2,1,0:T(8,128)(2,1)} %copy.130) | data formatting | bytes 6291456 | tf_op jit(solution)/shard_map/reshape | solution.py:224
  316.0 7.2 %copy.131 = bf16[64,2,12,1024]{3,1,2,0:T(2,128)(2,1)} copy(bf16[64,2,12,1024]{3,2,1,0:T(8,128)(2,1)} %reshape.127) | data formatting | bytes 6291456
  (78 shorter events, 36.0 us)
Async XLA Ops:
  7.2 7.4 %copy-start = (bf16[64,2,12,1024]{3,1,2,0:T(2,128)(2,1)S(1)}, bf16[64,2,12,1024]{3,1,2,0:T(2,128)(2,1)}, u32[]{:S(2)}) copy-start(bf16[64,2,12,1024]{3,1,2,0:T(2,128)(2,1)} %param.13) | copy-start | bytes 9437188
  7.2 8.0 %copy-start.10 = (s32[256,4]{0,1:T(4,128)S(1)}, s32[256,4]{0,1:T(4,128)}, u32[]{:S(2)}) copy-start(s32[256,4]{0,1:T(4,128)} %param.11) | copy-start | bytes 12292
  7.2 8.0 %copy-start.14 = (s32[64]{0:T(128)S(1)}, s32[64]{0:T(128)}, u32[]{:S(2)}) copy-start(s32[64]{0:T(128)} %param.12) | copy-start | bytes 772
  7.2 85.7 %all-gather.3.cloned.1.call-start = ((), (), s32[]{:S(2)}) async-start(), calls=%async_computation.5 | async-start | bytes 7077888 | tf_op jit(solution)/shard_map/all_gather | solution.py:157
  11.4 3.1 copy-start.12
  67.6 44.2 %all-to-all-start.1 = ((bf16[32,16,3072]{2,1,0:T(8,128)(2,1)}), bf16[32,16,3072]{2,1,0:T(8,128)(2,1)S(1)}, u32[]{:S(2)}, u32[]{:S(2)}) async-start(bf16[32,16,3072]{2,1,0:T(8,128)(2,1)} %get-tuple-element.41), calls=%async_computation.1 | async-start | bytes 6291456 | tf_op jit(solution)/shard_map/all_to_all | solution.py:173
  95.6 1.0 copy-start.5
  125.5 45.3 %all-to-all-start.2 = ((bf16[32,16,3072]{2,1,0:T(8,128)(2,1)}), bf16[32,16,3072]{2,1,0:T(8,128)(2,1)}, u32[]{:S(2)}, u32[]{:S(2)}) async-start(bf16[32,16,3072]{2,1,0:T(8,128)(2,1)} %reshape.120), calls=%async_computation.2 | async-start | bytes 6291456 | tf_op jit(solution)/shard_map/all_to_all | solution.py:212
  131.0 114.8 %reduce-scatter.2.cloned.1.call-start = ((), (), s32[]{:S(2)}) async-start(), calls=%async_computation.6 | async-start | bytes 7077888 | tf_op jit(solution)/shard_map/reduce_scatter | solution.py:209
  143.0 1.0 copy-start.7
  143.9 2.4 copy-start.3
  151.7 3.5 %copy-start.4 = (bf16[16,1,384,128]{3,0,2,1:T(8,128)(2,1)S(1)}, bf16[16,1,384,128]{3,0,2,1:T(8,128)(2,1)}, u32[]{:S(2)}) copy-start(bf16[16,1,384,128]{3,0,2,1:T(8,128)(2,1)} %get-tuple-element.44) | copy-start | bytes 4718596
  151.7 3.5 %copy-start.8 = (f32[16,128,128]{2,1,0:T(8,128)S(1)}, f32[16,128,128]{2,1,0:T(8,128)}, u32[]{:S(2)}) copy-start(f32[16,128,128]{2,1,0:T(8,128)} %copy-done.7) | copy-start | bytes 3145732
  155.2 1.4 copy-start.2
  155.2 1.7 copy-start.6
  185.0 44.6 %all-to-all-start.3 = ((bf16[32,16,3072]{2,1,0:T(8,128)(2,1)}), bf16[32,16,3072]{2,1,0:T(8,128)(2,1)S(1)}, u32[]{:S(2)}, u32[]{:S(2)}) async-start(bf16[32,16,3072]{2,1,0:T(8,128)(2,1)} %reshape.122), calls=%async_computation.3 | async-start | bytes 6291456 | tf_op jit(solution)/shard_map/all_to_all | solution.py:212
  189.9 108.5 %all-gather.5.cloned.1.call-start = ((), (), s32[]{:S(2)}) async-start(), calls=%async_computation.7 | async-start | bytes 3538944 | tf_op jit(solution)/shard_map/all_gather | solution.py:223
  193.4 53.7 %copy-start.11 = (s32[512]{0:T(512)S(1)}, s32[512]{0:T(512)}, u32[]{:S(2)}) copy-start(s32[512]{0:T(512)} %eq.103) | copy-start | bytes 6148
  249.9 4.9 %copy-start.13 = (s32[256,1]{0,1:T(1,128)S(1)}, s32[256,1]{0,1:T(1,128)}, u32[]{:S(2)}) copy-start(s32[256,1]{0,1:T(1,128)} %copy-done.12) | copy-start | bytes 3076
  252.9 4.6 %copy-start.9 = (f32[4,128,384]{2,1,0:T(8,128)S(1)}, f32[4,128,384]{2,1,0:T(8,128)}, u32[]{:S(2)}) copy-start(f32[4,128,384]{2,1,0:T(8,128)} %reduce-scatter.2.cloned.1.call-done) | copy-start | bytes 2359300
  309.0 14.2 %copy-start.1 = (bf16[64,2,12,1024]{3,1,2,0:T(2,128)(2,1)S(1)}, bf16[64,2,12,1024]{3,1,2,0:T(2,128)(2,1)}, u32[]{:S(2)}) copy-start(bf16[64,2,12,1024]{3,1,2,0:T(2,128)(2,1)} %param.13) | copy-start | bytes 9437188
Sparse Core Ops, SparseCore 0:
  14.6 78.2 all-gather.2
  171.0 74.7 reduce-scatter.1
  255.0 43.3 all-gather.4
